TPU v7x, 32 devices: a whole 2x2x4 slice. The times are simulated.
32 devices in a mesh: grp: 2 (over y), row: 8 (over z, core), col: 2 (over x).
Axes of the slice: x: 2, y: 2, z: 4, core: 2. Of those that a mesh axis runs over, the one named last changes fastest.
Arguments:
- pair: bfloat16 [192, 96, 128], P(('grp', 'row'), 'col'), parts along dimension 0, may hold values from -6 to 6
- token_count: int32 [2], P('grp'), parts along dimension 0, may hold values from 72 to 96
- tri_in: bfloat16 [2, 128, 512], replicated, may hold values from -0.5 to 0.5
- tri_gate: bfloat16 [2, 128, 128], replicated, may hold values from -0.5 to 0.5
- tri_out: bfloat16 [2, 128, 128], replicated, may hold values from -0.5 to 0.5
- trans_in: bfloat16 [128, 1024], replicated, may hold values from -0.5 to 0.5
- trans_out: bfloat16 [512, 128], replicated, may hold values from -0.25 to 0.25
Outputs:
- pair_out: bfloat16 [192, 96, 128], P(('grp', 'row'), 'col'), parts along dimension 0
There are 2 independent parts, one for each index of `grp`. A program takes and returns all parts, laid end to end along the dimension named above; an argument that names none is the same for every part. Nothing has to cross between parts.
Inputs may be any that keep to these rules, and one draw needn't show every extreme that they name: `token_count`: the number of real tokens of the complex; pair entries with either token index at or past it are padding.
All inputs are finite; a program needn't handle non-finite values.
Results may differ from a plain program's by a relative error of at most 0.015.
Values may be sent and summed in bfloat16 or wider, within the bound.
No kernel may reach another device: no remote copies, remote signals or barrier semaphores. Data moves between devices by JAX's collectives and lax.ppermute only.
A program may use at most 64 MiB of HBM per device.

v0:
```python
import jax
import jax.numpy as jnp
from jax import lax
from jax.sharding import PartitionSpec as P


def layer_norm(values, along):
    average = jnp.mean(values, axis=along, keepdims=True)
    centred = values - average
    spread = jnp.mean(centred * centred, axis=along, keepdims=True)
    return centred * lax.rsqrt(spread + 1e-05)


def contract_rows(left_side, right_side):
    return jnp.einsum("hik,hjk->hij", left_side, right_side, preferred_element_type=jnp.float32)


def contract_columns(left_side, right_side):
    return jnp.einsum("hki,hkj->hij", left_side, right_side, preferred_element_type=jnp.float32)


def body(pair, token_count, tri_in, tri_gate, tri_out, trans_in, trans_out):
    tile_rows, tile_cols, pair_width = pair.shape
    hidden = tri_out.shape[1]
    ffn_width = trans_out.shape[0]
    row_place = lax.axis_index("row")
    col_place = lax.axis_index("col")
    row_first = row_place * tile_rows
    col_first = col_place * tile_cols
    token_limit = token_count[0]
    row_keep = (row_first + jnp.arange(tile_rows, dtype=jnp.int32) < token_limit).astype(
        jnp.float32
    )
    col_keep = (col_first + jnp.arange(tile_cols, dtype=jnp.int32) < token_limit).astype(
        jnp.float32
    )
    keep_mask = row_keep[:, None] * col_keep[None, :]

    def project(stream, which_side):
        normed = layer_norm(stream.astype(jnp.float32), 2).astype(jnp.bfloat16)
        weight = tri_in[which_side].reshape(pair_width, 4, hidden)
        projected = jnp.einsum("ijc,cgh->ghij", normed, weight, preferred_element_type=jnp.float32)
        left_side = (keep_mask * jax.nn.sigmoid(projected[2]) * projected[0]).astype(jnp.bfloat16)
        right_side = (keep_mask * jax.nn.sigmoid(projected[3]) * projected[1]).astype(jnp.bfloat16)
        gate_value = jax.nn.sigmoid(
            jnp.dot(normed, tri_gate[which_side], preferred_element_type=jnp.float32)
        )
        return (left_side, right_side, gate_value)

    def finish(stream, mixed_sum, gate_value, which_side):
        normed = layer_norm(mixed_sum, 0).astype(jnp.bfloat16)
        update = gate_value * jnp.einsum(
            "hij,hc->ijc", normed, tri_out[which_side], preferred_element_type=jnp.float32
        )
        return (stream.astype(jnp.float32) + keep_mask[:, :, None] * update).astype(jnp.bfloat16)

    left_side, right_side, gate_value = project(pair, 0)
    partial_rows = contract_rows(left_side, lax.all_gather(right_side, "row", axis=1, tiled=True))
    mixed_sum = lax.psum_scatter(partial_rows, "col", scatter_dimension=2, tiled=True)
    stream = finish(pair, mixed_sum, gate_value, 0)
    left_side, right_side, gate_value = project(stream, 1)
    left_rows = lax.all_gather(left_side, "col", axis=2, tiled=True)
    column_strip = lax.all_to_all(left_rows, "row", split_axis=2, concat_axis=1, tiled=True)
    mixed_sum = contract_columns(
        column_strip, lax.all_gather(right_side, "row", axis=1, tiled=True)
    )
    stream = finish(stream, mixed_sum, gate_value, 1)
    normed = layer_norm(stream.astype(jnp.float32), 2).astype(jnp.bfloat16)
    inner_sum = jnp.dot(normed, trans_in, preferred_element_type=jnp.float32)
    activation = (jax.nn.silu(inner_sum[..., :ffn_width]) * inner_sum[..., ffn_width:]).astype(
        jnp.bfloat16
    )
    update = jnp.dot(activation, trans_out, preferred_element_type=jnp.float32)
    return (stream.astype(jnp.float32) + keep_mask[:, :, None] * update).astype(jnp.bfloat16)


def solution(mesh):
    placed = (P(("grp", "row"), "col", None), P("grp"), P(), P(), P(), P(), P())
    return jax.shard_map(
        body, mesh=mesh, in_specs=placed, out_specs=P(("grp", "row"), "col", None), check_vma=False
    )
```

profile of v0, /device:TPU:0, one launch (start us, length us, event | category | flops | bytes accessed | tf_op | source)
XLA Modules:
  0.0 121.3 jit_solution(946812768014044533)
XLA Ops:
  7.2 1.1 convert_reduce_fusion
  8.3 1.2 fusion.21
  9.5 1.6 %fusion.72 = (bf16[1,128,512]{2,1,0:T(8,128)(2,1)}, bf16[1,128,512]{2,1,0:T(8,128)(2,1)S(1)}) fusion(bf16[2,128,512]{2,1,0:T(8,128)(2,1)} %param.9), kind=kLoop, calls=%fused_computation.108 | loop fusion | bytes 524288 | tf_op jit(solution)/shard_map/slice | solution.py:41
  11.2 0.1 copy.110
  11.3 0.1 broadcast_multiply_fusion.5
  11.4 0.4 convolution_bitcast_fusion.1
  11.8 0.9 fusion.38
  12.7 0.0 all-gather.3.cloned.1.call-update
  12.7 0.0 reduce-scatter.2.cloned.1.call-start
  12.7 1.2 %copy.84 = bf16[128,12,48]{2,1,0:T(8,128)(2,1)} copy(bf16[128,12,48]{0,2,1:T(8,128)(2,1)S(1)} %get-tuple-element.8) | data formatting | bytes 294912 | tf_op jit(solution)/shard_map/convert_element_type | solution.py:43
  14.0 24.4 %all-gather.3.cloned.1.call-done = bf16[128,96,48]{0,2,1:T(8,128)(2,1)} async-done(((bf16[128,12,48]{0,2,1:T(8,128)(2,1)}), bf16[128,96,48]{0,2,1:T(8,128)(2,1)}) %all-gather.3.cloned.1.call-update) | async-done | bytes 1179664 | tf_op jit(solution)/shard_map/all_gather | solution.py:58
  38.3 5.3 %copy.85 = bf16[128,96,48]{2,1,0:T(8,128)(2,1)S(1)} copy(bf16[128,96,48]{0,2,1:T(8,128)(2,1)} %all-gather.3.cloned.1.call-done) | data formatting | bytes 2359296 | tf_op jit(solution)/shard_map/all_gather | solution.py:58
  43.6 3.7 %fusion.76 = f32[128,12,96]{2,1,0:T(8,128)} fusion(bf16[128,12,48]{2,1,0:T(8,128)(2,1)} %copy.84, bf16[128,96,48]{2,1,0:T(8,128)(2,1)S(1)} %copy.85), kind=kOutput, calls=%fused_computation.112 | convolution fusion | flops 14155776 | bytes 1916928 | tf_op jit(solution)/shard_map/hik,hjk->hij/dot_general | solution.py:15
  47.4 2.7 %copy.86 = f32[128,12,96]{0,1,2:T(8,128)} copy(f32[128,12,96]{2,1,0:T(8,128)} %fusion.76) | data formatting | bytes 1179648 | tf_op jit(solution)/shard_map/hik,hjk->hij/dot_general | solution.py:15
  50.1 0.0 reduce-scatter.2.cloned.1.call-update
  50.2 0.0 all-gather.5.cloned.1.call-start
  50.2 0.1 copy.114
  50.4 0.3 fusion.11
  50.7 16.7 %reduce-scatter.2.cloned.1.call-done = f32[128,12,48]{0,1,2:T(8,128)} async-done(((f32[128,12,96]{0,1,2:T(8,128)}), f32[128,12,48]{0,1,2:T(8,128)}) %reduce-scatter.2.cloned.1.call-update) | async-done | bytes 294928 | tf_op jit(solution)/shard_map/reduce_scatter | solution.py:59
  67.5 1.2 %reduce_sum.92 = f32[12,48]{0,1:T(8,128)S(1)} reduce(f32[128,12,48]{0,1,2:T(8,128)} %reduce-scatter.2.cloned.1.call-done, f32[]{:T(128)} %constant.32.clone.1), dimensions={0}, to_apply=%region_3.0 | reduce | flops 73152 | bytes 297220 | tf_op jit(solution)/shard_map/reduce_sum | solution.py:8
  68.7 0.1 copy.87
  68.8 0.1 copy.88
  68.9 1.3 %multiply_reduce_fusion.1 = f32[12,48]{0,1:T(8,128)S(1)} fusion(f32[128,12,48]{0,1,2:T(8,128)} %reduce-scatter.2.cloned.1.call-done, f32[12,48]{0,1:T(8,128)S(1)} %copy.88), kind=kLoop, calls=%fused_computation.31 | loop fusion | flops 220608 | bytes 299520 | tf_op jit(solution)/shard_map/reduce_sum | solution.py:10
  70.2 0.1 copy.89
  70.3 0.1 copy.90
  70.4 0.3 multiply_convert_fusion.1
  70.7 0.3 fusion.73
  71.0 0.3 multiply_reduce_fusion.3
  71.3 0.4 convolution_bitcast_fusion
  71.7 0.9 fusion.24
  72.6 6.1 %all_gather.10 = bf16[128,12,96]{0,2,1:T(8,128)(2,1)S(1)} all-gather(bf16[128,12,48]{0,2,1:T(8,128)(2,1)S(1)} %get-tuple-element.6), channel_id=1, replica_groups=mesh['grp'=2,'row'=8,'col'=2] {'col'}, dimensions={2}, use_global_device_ids=true | all-gather | bytes 442368 | tf_op jit(solution)/shard_map/all_gather | solution.py:62
  78.6 0.9 copy.95
  79.5 4.6 %all-to-all-start = ((bf16[128,12,96]{0,1,2:T(8,128)(2,1)}), bf16[128,12,96]{0,1,2:T(8,128)(2,1)S(1)}, u32[]{:S(2)}, u32[]{:S(2)}) async-start(bf16[128,12,96]{0,1,2:T(8,128)(2,1)} %copy.95), calls=%async_computation.1 | async-start | bytes 786432 | tf_op jit(solution)/shard_map/all_to_all | solution.py:63
  84.1 1.1 fusion.8
  85.2 17.1 %all-to-all-done = bf16[128,12,96]{0,1,2:T(8,128)(2,1)S(1)} async-done(((bf16[128,12,96]{0,1,2:T(8,128)(2,1)}), bf16[128,12,96]{0,1,2:T(8,128)(2,1)S(1)}, u32[]{:S(2)}, u32[]{:S(2)}) %all-to-all-start) | async-done | bytes 294944 | tf_op jit(solution)/shard_map/all_to_all | solution.py:63
  102.3 0.1 all_to_all.16
  102.4 1.2 %copy.98 = bf16[128,96,12]{1,2,0:T(8,128)(2,1)} copy(bf16[128,96,12]{0,1,2:T(8,128)(2,1)S(1)} %all_to_all.16) | data formatting | bytes 589824 | tf_op jit(solution)/shard_map/all_to_all | solution.py:63
  103.7 5.3 %copy.99 = bf16[128,96,48]{2,1,0:T(8,128)(2,1)S(1)} copy(bf16[128,96,48]{0,2,1:T(8,128)(2,1)} %all-gather.5.cloned.1.call-done) | data formatting | bytes 2359296 | tf_op jit(solution)/shard_map/all_gather | solution.py:65
  109.0 2.0 %fusion.74 = (f32[12,48]{1,0:T(8,128)S(1)}, f32[128,12,48]{2,1,0:T(8,128)S(1)}) fusion(bf16[128,96,12]{1,2,0:T(8,128)(2,1)} %copy.98, bf16[128,96,48]{2,1,0:T(8,128)(2,1)S(1)} %copy.99), kind=kOutput, calls=%fused_computation.110 | convolution fusion | flops 14228928 | bytes 1771776 | tf_op jit(solution)/shard_map/hki,hkj->hij/dot_general | solution.py:19
  111.0 0.2 multiply_reduce_fusion
  111.2 0.1 multiply_convert_fusion
  111.3 0.6 copy-done.2
  111.9 0.1 copy-done.6
  112.0 0.4 fusion.75
  112.4 0.3 multiply_reduce_fusion.2
  112.7 0.5 fusion.53
  113.3 0.4 copy-done.16
  113.6 1.1 fusion.14
  (49 shorter events, 0.2 us)
Async XLA Ops:
  6.5 106.2 %copy-start = (bf16[128,1024]{1,0:T(8,128)(2,1)S(1)}, bf16[128,1024]{1,0:T(8,128)(2,1)}, u32[]{:S(2)}) copy-start(bf16[128,1024]{1,0:T(8,128)(2,1)} %param.12) | copy-start | bytes 786436
  6.5 4.9 %copy-start.4 = (bf16[12,48,128]{2,1,0:T(8,128)(2,1)S(1)}, bf16[12,48,128]{2,1,0:T(8,128)(2,1)}, u32[]{:S(2)}) copy-start(bf16[12,48,128]{2,1,0:T(8,128)(2,1)} %param.7) | copy-start | bytes 442372
  6.5 31.8 %all-gather.3.cloned.1.call-start = ((), (), s32[]{:S(2)}) async-start(), calls=%async_computation.2 | async-start | bytes 1327104 | tf_op jit(solution)/shard_map/all_gather | solution.py:58
  8.3 3.5 %copy-start.10 = (f32[12,48]{1,0:T(8,128)}, f32[12,48]{1,0:T(8,128)S(1)}, u32[]{:S(2)}) copy-start(f32[12,48]{1,0:T(8,128)S(1)} %broadcast_multiply_fusion.4) | copy-start | bytes 6916
  9.5 3.1 %copy-start.14 = (f32[12,48]{1,0:T(8,128)}, f32[12,48]{1,0:T(8,128)S(1)}, u32[]{:S(2)}) copy-start(f32[12,48]{1,0:T(8,128)S(1)} %add_rsqrt_fusion.4) | copy-start | bytes 6916
  11.4 1.2 %copy-start.7 = (f32[12,48]{1,0:T(8,128)}, f32[12,48]{1,0:T(8,128)S(1)}, u32[]{:S(2)}) copy-start(f32[12,48]{1,0:T(8,128)S(1)} %broadcast_multiply_fusion.5) | copy-start | bytes 6916
  12.7 54.8 %reduce-scatter.2.cloned.1.call-start = ((), (), s32[]{:S(2)}) async-start(), calls=%async_computation.3 | async-start | bytes 1179648 | tf_op jit(solution)/shard_map/reduce_scatter | solution.py:59
  47.4 2.8 %copy-start.5 = (bf16[1,128,512]{2,1,0:T(8,128)(2,1)S(1)}, bf16[1,128,512]{2,1,0:T(8,128)(2,1)}, u32[]{:S(2)}) copy-start(bf16[1,128,512]{2,1,0:T(8,128)(2,1)} %get-tuple-element.9) | copy-start | bytes 393220
  47.4 2.9 %copy-start.11 = (f32[12,48]{1,0:T(8,128)S(1)}, f32[12,48]{1,0:T(8,128)}, u32[]{:S(2)}) copy-start(f32[12,48]{1,0:T(8,128)} %copy-done.10) | copy-start | bytes 6916
  47.4 2.9 %copy-start.15 = (f32[12,48]{1,0:T(8,128)S(1)}, f32[12,48]{1,0:T(8,128)}, u32[]{:S(2)}) copy-start(f32[12,48]{1,0:T(8,128)} %copy-done.14) | copy-start | bytes 6916
  47.4 3.0 %copy-start.17 = (bf16[2,128,128]{2,1,0:T(8,128)(2,1)S(1)}, bf16[2,128,128]{2,1,0:T(8,128)(2,1)}, u32[]{:S(2)}) copy-start(bf16[2,128,128]{2,1,0:T(8,128)(2,1)} %param.10) | copy-start | bytes 196612
  50.2 53.5 %all-gather.5.cloned.1.call-start = ((), (), s32[]{:S(2)}) async-start(), calls=%async_computation.4 | async-start | bytes 1327104 | tf_op jit(solution)/shard_map/all_gather | solution.py:65
  50.7 19.9 %copy-start.8 = (f32[12,48]{1,0:T(8,128)S(1)}, f32[12,48]{1,0:T(8,128)}, u32[]{:S(2)}) copy-start(f32[12,48]{1,0:T(8,128)} %copy-done.7) | copy-start | bytes 6916
  50.7 19.9 %copy-start.12 = (bf16[2,128,128]{2,1,0:T(8,128)(2,1)S(1)}, bf16[2,128,128]{2,1,0:T(8,128)(2,1)}, u32[]{:S(2)}) copy-start(bf16[2,128,128]{2,1,0:T(8,128)(2,1)} %param.11) | copy-start | bytes 196612
  67.5 2.9 %copy-start.3 = (f32[128,12,48]{0,1,2:T(8,128)S(1)}, f32[128,12,48]{0,1,2:T(8,128)}, u32[]{:S(2)}) copy-start(f32[128,12,48]{0,1,2:T(8,128)} %reduce-scatter.2.cloned.1.call-done) | copy-start | bytes 884740
  71.0 13.1 %copy-start.1 = (f32[12,48,128]{2,1,0:T(8,128)}, f32[12,48,128]{2,1,0:T(8,128)S(1)}, u32[]{:S(2)}) copy-start(f32[12,48,128]{2,1,0:T(8,128)S(1)} %get-tuple-element.12) | copy-start | bytes 884740
  79.5 22.8 %all-to-all-start = ((bf16[128,12,96]{0,1,2:T(8,128)(2,1)}), bf16[128,12,96]{0,1,2:T(8,128)(2,1)S(1)}, u32[]{:S(2)}, u32[]{:S(2)}) async-start(bf16[128,12,96]{0,1,2:T(8,128)(2,1)} %copy.95), calls=%async_computation.1 | async-start | bytes 786432 | tf_op jit(solution)/shard_map/all_to_all | solution.py:63
  111.0 1.0 copy-start.2
  111.0 1.0 copy-start.6
  111.0 1.0 copy-start.9
  111.0 1.0 copy-start.13
  112.7 0.9 copy-start.16
Sparse Core Ops, SparseCore 0:
  12.8 25.4 all-gather.2
  50.3 17.1 reduce-scatter.1
  72.7 30.0 all-gather.4
where the time goes:
time: 122 us; the launch traced here: 121 us
  waiting for transfers between devices  58.2 us (48%)
  local copies, waits for them, and re-layouts  20.1 us (16%)
  between operations  14.2 us (12%)
  matrix products  10.2 us (8%)
  other arithmetic  7.78 us (6%)
  blocking collectives  6.08 us (5%)
  starting transfers between devices  4.69 us (4%)
    all_gather x2, waiting for transfers between devices, body(): lax.all_gather(right_side, 'row', axis=1, tiled=True)  24.4 us
    all_to_all x1, waiting for transfers between devices, body(): lax.all_to_all(left_rows, 'row', split_axis=2, concat_axis=1, tiled=True)  17.1 us
    reduce_scatter x1, waiting for transfers between devices, body(): lax.psum_scatter(partial_rows, 'col', scatter_dimension=2, tiled=True)  16.7 us
    all_gather x2, local copies, waits for them, and re-layouts, body(): lax.all_gather(right_side, 'row', axis=1, tiled=True)  10.6 us
    all_gather x1, blocking collectives, body(): left_rows = lax.all_gather(left_side, 'col', axis=2, tiled=True)  6.08 us
    all_to_all x1, starting transfers between devices, body(): lax.all_to_all(left_rows, 'row', split_axis=2, concat_axis=1, tiled=True)  4.6 us
    dot_general x1, matrix products, contract_rows(): jnp.einsum('hik,hjk->hij', left_side, right_side, preferred_element_type=...  3.75 us
    reduce_sum x5, other arithmetic, layer_norm(): spread = jnp.mean(centred * centred, axis=along, keepdims=True)  3.23 us
  transfers between devices with their start and end apart: 4, of which 3 were waited for; matrix products, arithmetic and copies ran while one was open for 4% of the time, Pallas kernels for 0%

commit v1 on v0

v1 whole, which is shorter than its diff:
```python
import functools

import jax
import jax.numpy as jnp
from jax import lax
from jax.experimental import pallas as pl
from jax.experimental.pallas import tpu as pltpu
from jax.sharding import PartitionSpec as P


F32 = jnp.float32
VMEM_LIMIT = 24 * 1024 * 1024
BF16 = jnp.bfloat16


def norm(values):
    average = jnp.mean(values, axis=-1, keepdims=True)
    centred = values - average
    spread = jnp.mean(centred * centred, axis=-1, keepdims=True)
    return centred * lax.rsqrt(spread + 1e-05)


def dot(left, right):
    return jnp.dot(left, right, preferred_element_type=F32)


def keep_of(place, rows, cols, width):
    shape = (rows, cols, width)
    row = lax.broadcasted_iota(jnp.int32, shape, 0) + place[0]
    col = lax.broadcasted_iota(jnp.int32, shape, 1) + place[1]
    return jnp.where((row < place[2]) & (col < place[2]), 1.0, 0.0).astype(F32)


def gated(normed, weight, side, which, hidden):
    value = dot(normed, weight[side, :, which * hidden : (which + 1) * hidden])
    gate = dot(normed, weight[side, :, (which + 2) * hidden : (which + 3) * hidden])
    return jax.nn.sigmoid(gate) * value


def call(kernel, outs, *args, scratch=(), flops=2_000_000_000, space=pltpu.VMEM):
    nbytes = sum(a.size * a.dtype.itemsize for a in (*args[1:], *outs))
    return pl.pallas_call(
        kernel,
        out_shape=outs,
        in_specs=[pl.BlockSpec(memory_space=pltpu.SMEM)]
        + [pl.BlockSpec(memory_space=space)] * (len(args) - 1),
        out_specs=[pl.BlockSpec(memory_space=pltpu.VMEM)] * len(outs),
        scratch_shapes=scratch,
        cost_estimate=pl.CostEstimate(flops=flops, bytes_accessed=nbytes, transcendentals=0),
        compiler_params=pltpu.CompilerParams(vmem_limit_bytes=VMEM_LIMIT),
    )(*args)


def start_kernel(place, pair, weight, b_out, tile, value, gate, sems):
    rows, cols, width = pair.shape
    hidden = b_out.shape[2]
    copies = [
        pltpu.make_async_copy(source, target, sems.at[turn])
        for turn, (source, target) in enumerate(
            (
                (pair, tile),
                (weight.at[0, :, hidden : 2 * hidden], value),
                (weight.at[0, :, 3 * hidden :], gate),
            )
        )
    ]
    for copy in copies:
        copy.start()
    for copy in copies:
        copy.wait()
    normed = norm(tile[...].astype(F32)).astype(BF16).reshape(rows * cols, width)
    b = (jax.nn.sigmoid(dot(normed, gate[...])) * dot(normed, value[...])).reshape(rows, cols, hidden)
    b_out[...] = (keep_of(place, rows, cols, hidden) * b).astype(BF16)


def second_kernel(place, pair, weight, a_out):
    rows, cols, width = pair.shape
    hidden = a_out.shape[2]
    normed = norm(pair[...].astype(F32)).astype(BF16).reshape(rows * cols, width)
    a = gated(normed, weight, 0, 0, hidden).reshape(rows, cols, hidden)
    a_out[...] = (keep_of(place, rows, cols, hidden) * a).astype(BF16).astype(F32)


def gates_kernel(place, weight_gate, *refs):
    *tiles, pairs_out, gates_out = refs
    rows, cols, width = tiles[0].shape
    span = 2 * rows
    per = cols // span
    for step, tile in enumerate(tiles):
        wide = tile[...].astype(F32)
        for piece in range(per):
            cut = wide[:, piece * span : (piece + 1) * span, :].reshape(rows * span, width)
            pairs_out[step * per + piece] = cut
            gates_out[step * per + piece] = jax.nn.sigmoid(dot(norm(cut).astype(BF16), weight_gate[0]))


def mix_rows_kernel(send, place, a, b_same, b_other, *refs):
    earlier, (part_out, *send_out), wide = (refs[: max(send - 1, 0)], refs[max(send - 1, 0) : -1], refs[-1])
    rows = a.shape[0]
    step = 2 if rows % 2 == 0 else 1
    for swap, block in enumerate((b_same, b_other)):
        wide[...] = block[...].astype(F32)
        first = rows * (place[3] ^ swap)

        @pl.loop(0, rows // step)
        def _(turn):
            left = [a[turn * step + s] for s in range(step)]
            for j in range(rows):
                right = wide[j]
                for s in range(step):
                    total = jnp.sum(left[s] * right, axis=0, keepdims=True)
                    part_out[turn * step + s, pl.ds(first + j, 1), :] = total

    cut = part_out.shape[0] * part_out.shape[1]
    for turn, part in enumerate((*earlier, part_out) if send else ()):
        send_out[0][turn * cut : (turn + 1) * cut] = part[...].reshape(cut, part.shape[2]).astype(BF16)


def middle_kernel(step, per, which_cut, place, pairs, gates, weight_out, weight_in, part, *refs):
    *others, stream_out, ab_out = refs
    rows, span, hidden = part.shape
    width = pairs.shape[2]
    total = part[...].reshape(rows * span, hidden)
    for other in others:
        total = total + other[which_cut * rows * span : (which_cut + 1) * rows * span].astype(F32)
    group, piece = divmod(step, per)
    which = (place[4] ^ group) * per + (place[5] ^ piece)
    mixnorm = norm(total).astype(BF16)
    update = gates[which] * dot(mixnorm, weight_out[0])
    shape = (rows, span, width)
    row = lax.broadcasted_iota(jnp.int32, shape, 0) + place[0]
    col = lax.broadcasted_iota(jnp.int32, shape, 1) + (place[6] ^ step) * span
    keep = jnp.where((row < place[2]) & (col < place[2]), 1.0, 0.0).astype(F32).reshape(rows * span, width)
    stream = (pairs[which] + keep * update).astype(BF16)
    stream_out[...] = stream
    normed = norm(stream.astype(F32)).astype(BF16)
    for side in range(2):
        value = keep * gated(normed, weight_in, 1, side, hidden)
        ab_out[side] = value.reshape(rows, span, hidden).astype(BF16)


def mix_cols_kernel(per, step, place, *refs):
    same, other = refs[: (len(refs) - 3) // 2], refs[(len(refs) - 3) // 2 : -3]
    out, wide_a, wide_b = refs[-3:]
    _, rows, span, _ = same[0].shape
    for half, source in enumerate((same[step], other[step])):
        wide_a[half * rows : (half + 1) * rows] = source[0].astype(F32)
    for group in range(len(same) // per):

        @pl.when(place[4] == group)
        def _():
            for piece in range(per):
                first = pl.multiple_of((place[5] ^ piece) * span, 8)
                for half, source in enumerate((same, other)):
                    value = source[group * per + piece][1].astype(F32)
                    wide_b[half * rows : (half + 1) * rows, pl.ds(first, span), :] = value

    steps = 4 if rows % 4 == 0 else 1
    first = place[3] * rows

    @pl.loop(0, rows // steps)
    def _(turn):
        totals = [None] * steps
        for k in range(2 * rows):
            right = wide_b[k]
            for s in range(steps):
                row = wide_a[k, pl.ds(first + turn * steps + s, 1), :]
                term = row * right
                totals[s] = term if totals[s] is None else totals[s] + term
        for s in range(steps):
            out[turn * steps + s] = totals[s].astype(out.dtype)


def own_kernel(per, place, weight_gate, *refs):
    *pieces, stream_out, gate_out, wide = refs
    rows, cols, width = stream_out.shape
    span = 2 * rows
    for group in range(len(pieces) // per):

        @pl.when(place[4] == group)
        def _():
            for piece in range(per):
                first = pl.multiple_of((place[5] ^ piece) * span, 8)
                value = pieces[group * per + piece][...].astype(F32).reshape(rows, span, width)
                wide[:, pl.ds(first, span), :] = value

    stream = wide[...]
    stream_out[...] = stream.astype(BF16)
    normed = norm(stream).astype(BF16).reshape(rows * cols, width)
    gate_out[...] = jax.nn.sigmoid(dot(normed, weight_gate[1]))


def last_kernel(place, stream, gate, weight_out, trans_in, trans_out, own, *refs):
    others, (out,) = refs[:-1], refs[-1:]
    rows, cols, width = stream.shape
    total = own[...]
    for other in others:
        total = total + other[...].astype(F32)
    hidden = total.shape[2]
    mixnorm = norm(total.reshape(rows * cols, hidden)).astype(BF16)
    update = (gate[...] * dot(mixnorm, weight_out[1])).reshape(rows, cols, width)
    keep = keep_of(place, rows, cols, width)
    after = (stream[...].astype(F32) + keep * update).astype(BF16)
    normed = norm(after.astype(F32)).astype(BF16).reshape(rows * cols, width)
    ffn = trans_out.shape[0]
    inner = dot(normed, trans_in[:, :ffn])
    act = (jax.nn.silu(inner) * dot(normed, trans_in[:, ffn:])).astype(BF16)
    update = dot(act, trans_out[...]).reshape(rows, cols, width)
    out[...] = (after.astype(F32) + keep * update).astype(BF16)


def sequence(n_chip):
    return [0, 1, *range(n_chip - 1, 1, -1)]


def sending(n_chip):
    return [*range(min(2, n_chip - 1), n_chip), *range(min(2, n_chip - 1) - 1, -1, -1)]


def body(n_row, n_col, pair, token_count, tri_in, tri_gate, tri_out, trans_in, trans_out):
    rows, cols, width = pair.shape
    hidden = tri_out.shape[1]
    n_chip = n_row // 2
    per = n_chip // n_col
    span = 2 * rows
    row_place = lax.axis_index("row")
    col_place = lax.axis_index("col")
    chip = row_place // 2
    lane = jnp.arange(8, dtype=jnp.int32)
    values = (
        row_place * rows,
        col_place * cols,
        token_count[0],
        row_place % 2,
        (chip // per) ^ col_place,
        chip % per,
        chip,
    )
    place = jnp.zeros((8,), jnp.int32)
    for where, value in enumerate(values):
        place = jnp.where(lane == where, value, place)

    def along_row(value, mask):
        return lax.ppermute(value, "row", [(i, i ^ mask) for i in range(n_row)])

    def along_col(value, mask):
        return lax.ppermute(value, "col", [(i, i ^ mask) for i in range(n_col)])

    def shape(*extent, dtype=BF16):
        return jax.ShapeDtypeStruct(extent, dtype)

    tile = (rows, cols, hidden)
    cut = (rows * span, width)
    tiles = [pair] + [along_col(pair, step) for step in range(1, n_col)]
    (b,) = call(
        start_kernel,
        [shape(*tile)],
        place,
        pltpu.with_memory_space_constraint(pair, pltpu.HBM),
        pltpu.with_memory_space_constraint(tri_in, pltpu.HBM),
        scratch=[
            pltpu.VMEM((rows, cols, width), BF16),
            pltpu.VMEM((width, hidden), BF16),
            pltpu.VMEM((width, hidden), BF16),
            pltpu.SemaphoreType.DMA((3,)),
        ],
        space=pltpu.HBM,
    )
    turns = sequence(n_chip)
    arrived = {0: b}
    for step in turns[1:]:
        arrived[step] = along_row(b, 2 * step)
    (a,) = call(second_kernel, [shape(*tile, dtype=F32)], place, pair, tri_in)
    pairs, gates = call(gates_kernel, [shape(n_chip, *cut, dtype=F32)] * 2, place, tri_gate, *tiles)
    streams, same, other = ({}, {}, {})
    parts = {}
    joined = turns[:2]
    for step in turns:
        block = arrived[step]
        send = {joined[0]: 0, joined[1]: 2}.get(step, 1)
        parts[step], *sent = call(
            functools.partial(mix_rows_kernel, send),
            [shape(rows, span, hidden, dtype=F32)] + [shape(send * rows * span, hidden)] * (send > 0),
            place,
            a,
            block,
            along_row(block, 1),
            *[parts[before] for before in joined[:1] if send > 1],
            scratch=[pltpu.VMEM(tile, F32)],
        )
        if not send:
            continue
        sent = [along_col(sent[0], mask) for mask in range(1, n_col)]
        for which, ready in enumerate(joined if send > 1 else [step]):
            streams[ready], same[ready] = call(
                functools.partial(middle_kernel, ready, per, which),
                [shape(*cut), shape(2, rows, span, hidden)],
                place,
                pairs,
                gates,
                tri_out,
                tri_in,
                parts[ready],
                *sent,
            )
            other[ready] = along_row(same[ready], 1)
    totals = {}
    streams, same, other = ([values[step] for step in range(n_chip)] for values in (streams, same, other))
    for step in sending(n_chip):
        (out,) = call(
            functools.partial(mix_cols_kernel, per, step),
            [shape(*tile, dtype=BF16 if step else F32)],
            place,
            *same,
            *other,
            scratch=[pltpu.VMEM((span, span, hidden), F32), pltpu.VMEM((span, cols, hidden), F32)],
        )
        totals[step] = along_row(out, 2 * step) if step else out
    stream, gate = call(
        functools.partial(own_kernel, per),
        [shape(rows, cols, width), shape(rows * cols, width, dtype=F32)],
        place,
        tri_gate,
        *streams,
        scratch=[pltpu.VMEM((rows, cols, width), F32)],
    )
    (out,) = call(
        last_kernel,
        [shape(rows, cols, width)],
        place,
        stream,
        gate,
        tri_out,
        trans_in,
        trans_out,
        *[totals[step] for step in range(n_chip)],
    )
    return out


def solution(mesh):
    placed = (P(("grp", "row"), "col", None), P("grp"), P(), P(), P(), P(), P())

    def step(*args):
        return body(mesh.shape["row"], mesh.shape["col"], *args)

    return jax.shard_map(
        step,
        mesh=mesh,
        in_specs=placed,
        out_specs=P(("grp", "row"), "col", None),
        check_vma=False,
    )
```

time: 122 us -> 58.7 us (0.48)
  waiting for transfers between devices: 58.2 us -> 17.8 us
  Pallas kernels: 0 us -> 22.2 us
  local copies, waits for them, and re-layouts: 20.1 us -> 0.04 us
  between operations: 14.2 us -> 0.88 us
  starting transfers between devices: 4.69 us -> 17.5 us
  matrix products: 10.2 us -> 0 us
  other arithmetic: 7.78 us -> 0.01 us
  blocking collectives: 6.08 us -> 0 us
    all_gather x2 -> x0, waiting for transfers between devices: 24.4 us -> none  [body(): lax.all_gather(right_side, 'row', axis=1, tiled=True)]
    pallas_call x0 -> x17, Pallas kernels: none -> 22.2 us  [call(): pl.pallas_call(kernel, out_shape=outs, in_specs=[pl.BlockSpec(memory_spac...]
    ppermute x0 -> x18, waiting for transfers between devices: none -> 17.8 us  [the longest x14 16.6 us: along_row(): return lax.ppermute(value, 'row', [(i, i ^ mask) for i in range(n_row)])]
    ppermute x0 -> x18, starting transfers between devices: none -> 17.5 us  [the longest x14 12.1 us: along_row(): return lax.ppermute(value, 'row', [(i, i ^ mask) for i in range(n_row)])]
    all_to_all x1 -> x0, waiting for transfers between devices: 17.1 us -> none  [body(): lax.all_to_all(left_rows, 'row', split_axis=2, concat_axis=1, tiled=True)]
    reduce_scatter x1 -> x0, waiting for transfers between devices: 16.7 us -> none  [body(): lax.psum_scatter(partial_rows, 'col', scatter_dimension=2, tiled=True)]
    all_gather x3 -> x0, local copies, waits for them, and re-layouts: 11.5 us -> none  [the longest x2 10.6 us: body(): lax.all_gather(right_side, 'row', axis=1, tiled=True)]
    dot_general x10 -> x0, matrix products: 10.2 us -> none  [the longest x1 3.75 us: contract_rows(): jnp.einsum('hik,hjk->hij', left_side, right_side, preferred_element_type=...]
  transfers between devices with their start and end apart: 4 -> 18, of which waited for: 3 -> 4; matrix products, arithmetic and copies ran while one was open for 4% -> 0% of each run, Pallas kernels for 0% -> 29%
where the time goes in v1:
time: 58.7 us; the launch traced here: 58.4 us
  Pallas kernels  22.2 us (38%)
  waiting for transfers between devices  17.8 us (30%)
  starting transfers between devices  17.5 us (30%)
  between operations  0.88 us (1%)
    pallas_call x17, Pallas kernels, call(): pl.pallas_call(kernel, out_shape=outs, in_specs=[pl.BlockSpec(memory_spac...  22.2 us
    ppermute x14, waiting for transfers between devices, along_row(): return lax.ppermute(value, 'row', [(i, i ^ mask) for i in range(n_row)])  16.6 us
    ppermute x14, starting transfers between devices, along_row(): return lax.ppermute(value, 'row', [(i, i ^ mask) for i in range(n_row)])  12.1 us
    ppermute x4, starting transfers between devices, along_col(): return lax.ppermute(value, 'col', [(i, i ^ mask) for i in range(n_col)])  5.35 us
    ppermute x4, waiting for transfers between devices, along_col(): return lax.ppermute(value, 'col', [(i, i ^ mask) for i in range(n_col)])  1.27 us
  transfers between devices with their start and end apart: 18, of which 4 were waited for; matrix products, arithmetic and copies ran while one was open for 0% of the time, Pallas kernels for 29%

profile of v1, /device:TPU:0, one launch (start us, length us, event | category | flops | bytes accessed | tf_op | source)
XLA Modules:
  0.0 58.4 jit_solution(7821951626901014781)
XLA Ops:
  0.7 0.0 copy-start.2
  0.7 0.0 copy-start
  0.7 1.9 %shard_map.75.b_same = bf16[12,48,128]{2,1,0:T(8,128)(2,1)S(1)} custom-call(s32[8]{0:T(128)S(1)} %compare_select_fusion.6.place, bf16[12,48,128]{2,1,0:T(8,128)(2,1)} %pair.3, bf16[2,128,512]{2,1,0:T(8,128)(2,1)} %weight_in.7), custom_call_target="tpu_custom_call" | custom-call | flops 2000000000 | bytes 557056 | tf_op jit(solution)/shard_map/pallas_call | solution.py:42
  2.6 5.1 %collective-permute-start.8 = (bf16[12,48,128]{2,1,0:T(8,128)(2,1)S(1)}, bf16[12,48,128]{2,1,0:T(8,128)(2,1)S(1)}, u32[]{:S(2)}, u32[]{:S(2)}) collective-permute-start(bf16[12,48,128]{2,1,0:T(8,128)(2,1)S(1)} %shard_map.75.b_same), channel_id=1, source_target_pairs={{0,12},{2,14},{4,8},{6,10},{8,4},{10,6},{12,0},{14,2},{1,13},{3,15... | collective-permute-start | bytes 442376 | tf_op jit(solution)/shard_map/ppermute | solution.py:244
  7.8 0.0 collective-permute-start.5
  7.8 0.6 %collective-permute-start.2 = (bf16[12,48,128]{2,1,0:T(8,128)(2,1)S(1)}, bf16[12,48,128]{2,1,0:T(8,128)(2,1)S(1)}, u32[]{:S(2)}, u32[]{:S(2)}) collective-permute-start(bf16[12,48,128]{2,1,0:T(8,128)(2,1)S(1)} %shard_map.75.b_same), channel_id=1, source_target_pairs={{0,4},{2,6},{4,0},{6,2},{8,12},{10,14},{12,8},{14,10},{1,5},{3,7},... | collective-permute-start | bytes 442376 | tf_op jit(solution)/shard_map/ppermute | solution.py:244
  8.4 0.0 collective-permute-start.1
  8.4 1.6 %collective-permute-start = (bf16[12,48,128]{2,1,0:T(8,128)(2,1)S(1)}, bf16[12,48,128]{2,1,0:T(8,128)(2,1)S(1)}, u32[]{:S(2)}, u32[]{:S(2)}) collective-permute-start(bf16[12,48,128]{2,1,0:T(8,128)(2,1)S(1)} %copy-done.2), channel_id=1, source_target_pairs={{0,1},{1,0},{2,3},{3,2},{4,5},{5,4},{6,7},{7,6},{8,9},{9,8},{10,11... | collective-permute-start | bytes 442376 | tf_op jit(solution)/shard_map/ppermute | solution.py:247
  10.0 1.0 %shard_map.74.a = f32[12,48,128]{2,1,0:T(8,128)S(1)} custom-call(s32[8]{0:T(128)S(1)} %compare_select_fusion.6.place, bf16[12,48,128]{2,1,0:T(8,128)(2,1)S(1)} %copy-done.2, bf16[2,128,512]{2,1,0:T(8,128)(2,1)S(1)} %copy-done), custom_call_target="tpu_custom_call" | custom-call | flops 2000000000 | bytes 704512 | tf_op jit(solution)/shard_map/pallas_call | solution.py:42
  11.0 0.0 copy-start.4
  11.0 1.5 %collective-permute-done.8.b_same = bf16[12,48,128]{2,1,0:T(8,128)(2,1)S(1)} collective-permute-done((bf16[12,48,128]{2,1,0:T(8,128)(2,1)S(1)}, bf16[12,48,128]{2,1,0:T(8,128)(2,1)S(1)}, u32[]{:S(2)}, u32[]{:S(2)}) %collective-permute-start.8) | collective-permute-done | bytes 147488 | tf_op jit(solution)/shard_map/ppermute | solution.py:244
  12.6 0.0 collective-permute-start.9
  12.6 7.7 %collective-permute-done.5.b_same = bf16[12,48,128]{2,1,0:T(8,128)(2,1)S(1)} collective-permute-done((bf16[12,48,128]{2,1,0:T(8,128)(2,1)S(1)}, bf16[12,48,128]{2,1,0:T(8,128)(2,1)S(1)}, u32[]{:S(2)}, u32[]{:S(2)}) %collective-permute-start.5) | collective-permute-done | bytes 147488 | tf_op jit(solution)/shard_map/ppermute | solution.py:244
  20.2 0.0 collective-permute-done.2.b_same
  20.2 0.5 collective-permute-start.3
  20.8 0.0 collective-permute-done.1.b_other
  20.8 1.3 %shard_map.76.refs_0_.part = f32[12,24,128]{2,1,0:T(8,128)S(1)} custom-call(s32[8]{0:T(128)S(1)} %compare_select_fusion.6.place, f32[12,48,128]{2,1,0:T(8,128)S(1)} %shard_map.74.a, bf16[12,48,128]{2,1,0:T(8,128)(2,1)S(1)} %shard_map.75.b_same, bf16[12,48,128]{2,1,0:T(8,128)(2,1)S(1)} %collective-permute-done.1.b_other), custom_call_target="tpu_custom_call" | custom-call | flops 2000000000 | bytes 737280 | tf_op jit(solution)/shard_map/pallas_call | solution.py:42
  22.1 0.0 collective-permute-done.refs_1_
  22.1 1.1 %shard_map.73 = (f32[4,288,128]{2,1,0:T(8,128)S(1)}, f32[4,288,128]{2,1,0:T(8,128)S(1)}) custom-call(s32[8]{0:T(128)S(1)} %compare_select_fusion.6.place, bf16[2,128,128]{2,1,0:T(8,128)(2,1)S(1)} %copy-done.4, bf16[12,48,128]{2,1,0:T(8,128)(2,1)S(1)} %copy-done.2, bf16[12,48,128]{2,1,0:T(8,128)(2,1)S(1)} %collective-permute-done.refs_1_), custom_call_target="tpu_custom_call" | custom-call | flops 2000000000 | bytes 1540096 | tf_op jit(solution)/shard_map/pallas_call | solution.py:42
  23.2 1.3 %shard_map.82 = (f32[12,24,128]{2,1,0:T(8,128)S(1)}, bf16[288,128]{1,0:T(8,128)(2,1)S(1)}) custom-call(s32[8]{0:T(128)S(1)} %compare_select_fusion.6.place, f32[12,48,128]{2,1,0:T(8,128)S(1)} %shard_map.74.a, bf16[12,48,128]{2,1,0:T(8,128)(2,1)S(1)} %collective-permute-done.8.b_same, bf16[12,48,128]{2,1,0:T(8,128)(2,1)S(1)} %collective-permute-done.9.b_other), custom_call_target="tpu_custom_call" | custom-call | flops 2000000000 | bytes 811008 | tf_op jit(solution)/shard_map/pallas_call | solution.py:42
  24.5 1.6 %collective-permute-start.10 = (bf16[288,128]{1,0:T(8,128)(2,1)S(1)}, bf16[288,128]{1,0:T(8,128)(2,1)S(1)}, u32[]{:S(2)}, u32[]{:S(2)}) collective-permute-start(bf16[288,128]{1,0:T(8,128)(2,1)S(1)} %get-tuple-element.33), channel_id=1, source_target_pairs={{0,1},{1,0},{2,3},{3,2},{4,5},{5,4},{6,7},{7,6},{8,9},{9,8},{10,11... | collective-permute-start | bytes 221192 | tf_op jit(solution)/shard_map/ppermute | solution.py:247
  26.1 1.3 %shard_map.80 = (f32[12,24,128]{2,1,0:T(8,128)S(1)}, bf16[288,128]{1,0:T(8,128)(2,1)S(1)}) custom-call(s32[8]{0:T(128)S(1)} %compare_select_fusion.6.place, f32[12,48,128]{2,1,0:T(8,128)S(1)} %shard_map.74.a, bf16[12,48,128]{2,1,0:T(8,128)(2,1)S(1)} %collective-permute-done.5.b_same, bf16[12,48,128]{2,1,0:T(8,128)(2,1)S(1)} %collective-permute-done.6.b_other), custom_call_target="tpu_custom_call" | custom-call | flops 2000000000 | bytes 811008 | tf_op jit(solution)/shard_map/pallas_call | solution.py:42
  27.4 0.0 copy-start.5
  27.5 0.6 %collective-permute-start.7 = (bf16[288,128]{1,0:T(8,128)(2,1)S(1)}, bf16[288,128]{1,0:T(8,128)(2,1)S(1)}, u32[]{:S(2)}, u32[]{:S(2)}) collective-permute-start(bf16[288,128]{1,0:T(8,128)(2,1)S(1)} %get-tuple-element.30), channel_id=1, source_target_pairs={{0,1},{1,0},{2,3},{3,2},{4,5},{5,4},{6,7},{7,6},{8,9},{9,8},{10,11... | collective-permute-start | bytes 221192 | tf_op jit(solution)/shard_map/ppermute | solution.py:247
  28.1 1.3 %shard_map.77 = (f32[12,24,128]{2,1,0:T(8,128)S(1)}, bf16[576,128]{1,0:T(8,128)(2,1)S(1)}) custom-call(s32[8]{0:T(128)S(1)} %compare_select_fusion.6.place, f32[12,48,128]{2,1,0:T(8,128)S(1)} %shard_map.74.a, bf16[12,48,128]{2,1,0:T(8,128)(2,1)S(1)} %collective-permute-done.2.b_same, bf16[12,48,128]{2,1,0:T(8,128)(2,1)S(1)} %collective-permute-done.3.b_other, ...), custom_call_target="tpu_custom_call" | custom-call | flops 2000000000 | bytes 1032192 | tf_op jit(solution)/shard_map/pallas_call | solution.py:42
  29.4 1.6 %collective-permute-start.4 = (bf16[576,128]{1,0:T(8,128)(2,1)S(1)}, bf16[576,128]{1,0:T(8,128)(2,1)S(1)}, u32[]{:S(2)}, u32[]{:S(2)}) collective-permute-start(bf16[576,128]{1,0:T(8,128)(2,1)S(1)} %get-tuple-element.25), channel_id=1, source_target_pairs={{0,1},{1,0},{2,3},{3,2},{4,5},{5,4},{6,7},{7,6},{8,9},{9,8},{10,11... | collective-permute-start | bytes 442376 | tf_op jit(solution)/shard_map/ppermute | solution.py:247
  31.0 1.3 %collective-permute-done.7.refs_0_ = bf16[288,128]{1,0:T(8,128)(2,1)S(1)} collective-permute-done((bf16[288,128]{1,0:T(8,128)(2,1)S(1)}, bf16[288,128]{1,0:T(8,128)(2,1)S(1)}, u32[]{:S(2)}, u32[]{:S(2)}) %collective-permute-start.7) | collective-permute-done | bytes 73760 | tf_op jit(solution)/shard_map/ppermute | solution.py:247
  32.2 1.2 %shard_map.81 = (bf16[288,128]{1,0:T(8,128)(2,1)S(1)}, bf16[2,12,24,128]{3,2,1,0:T(8,128)(2,1)S(1)}) custom-call(s32[8]{0:T(128)S(1)} %compare_select_fusion.6.place, f32[4,288,128]{2,1,0:T(8,128)S(1)} %get-tuple-element.23.pairs, f32[4,288,128]{2,1,0:T(8,128)S(1)} %get-tuple-element.24.gates, bf16[2,128,128]{2,1,0:T(8,128)(2,1)S(1)} %copy-done.5, ...), custom_call_target="tpu_custom_call" | custom-call | flops 2000000000 | bytes 1949696 | tf_op jit(solution)/shard_map/pallas_call | solution.py:42
  33.5 0.1 collective-permute-start.13
  33.5 1.2 %shard_map.83 = (bf16[288,128]{1,0:T(8,128)(2,1)S(1)}, bf16[2,12,24,128]{3,2,1,0:T(8,128)(2,1)S(1)}) custom-call(s32[8]{0:T(128)S(1)} %compare_select_fusion.6.place, f32[4,288,128]{2,1,0:T(8,128)S(1)} %get-tuple-element.23.pairs, f32[4,288,128]{2,1,0:T(8,128)S(1)} %get-tuple-element.24.gates, bf16[2,128,128]{2,1,0:T(8,128)(2,1)S(1)} %copy-done.5, ...), custom_call_target="tpu_custom_call" | custom-call | flops 2000000000 | bytes 1949696 | tf_op jit(solution)/shard_map/pallas_call | solution.py:42
  34.8 0.6 collective-permute-start.14
  35.3 1.2 %shard_map.79 = (bf16[288,128]{1,0:T(8,128)(2,1)S(1)}, bf16[2,12,24,128]{3,2,1,0:T(8,128)(2,1)S(1)}) custom-call(s32[8]{0:T(128)S(1)} %compare_select_fusion.6.place, f32[4,288,128]{2,1,0:T(8,128)S(1)} %get-tuple-element.23.pairs, f32[4,288,128]{2,1,0:T(8,128)S(1)} %get-tuple-element.24.gates, bf16[2,128,128]{2,1,0:T(8,128)(2,1)S(1)} %copy-done.5, ...), custom_call_target="tpu_custom_call" | custom-call | flops 2000000000 | bytes 2023424 | tf_op jit(solution)/shard_map/pallas_call | solution.py:42
  36.6 0.1 collective-permute-start.12
  36.6 1.2 %shard_map.78 = (bf16[288,128]{1,0:T(8,128)(2,1)S(1)}, bf16[2,12,24,128]{3,2,1,0:T(8,128)(2,1)S(1)}) custom-call(s32[8]{0:T(128)S(1)} %compare_select_fusion.6.place, f32[4,288,128]{2,1,0:T(8,128)S(1)} %get-tuple-element.23.pairs, f32[4,288,128]{2,1,0:T(8,128)S(1)} %get-tuple-element.24.gates, bf16[2,128,128]{2,1,0:T(8,128)(2,1)S(1)} %copy-done.5, ...), custom_call_target="tpu_custom_call" | custom-call | flops 2000000000 | bytes 2023424 | tf_op jit(solution)/shard_map/pallas_call | solution.py:42
  37.9 0.6 collective-permute-start.11
  38.4 0.9 %shard_map.84 = (bf16[12,48,128]{2,1,0:T(8,128)(2,1)S(1)}, f32[576,128]{1,0:T(8,128)S(1)}) custom-call(s32[8]{0:T(128)S(1)} %compare_select_fusion.6.place, bf16[2,128,128]{2,1,0:T(8,128)(2,1)S(1)} %copy-done.4, bf16[288,128]{1,0:T(8,128)(2,1)S(1)} %get-tuple-element.26.refs_0_, bf16[288,128]{1,0:T(8,128)(2,1)S(1)} %get-tuple-element.28.refs_1_, ...), custom_call_target="tpu_custom_call" | custom-call | flops 2000000000 | bytes 802816 | tf_op jit(solution)/shard_map/pallas_call | solution.py:42
  39.4 0.0 collective-permute-done.11.refs_4_
  39.4 1.2 %shard_map.86 = bf16[12,48,128]{2,1,0:T(8,128)(2,1)S(1)} custom-call(s32[8]{0:T(128)S(1)} %compare_select_fusion.6.place, bf16[2,12,24,128]{3,2,1,0:T(8,128)(2,1)S(1)} %get-tuple-element.37.refs_0_, bf16[2,12,24,128]{3,2,1,0:T(8,128)(2,1)S(1)} %get-tuple-element.38.refs_1_, bf16[2,12,24,128]{3,2,1,0:T(8,128)(2,1)S(1)} %get-tuple-element.39.refs_2_, ...), custom_call_target="tpu_custom_call" | custom-call | flops 2000000000 | bytes 1327104 | tf_op jit(solution)/shard_map/pallas_call | solution.py:42
  40.6 0.1 collective-permute-start.15
  40.7 1.2 %shard_map.87 = bf16[12,48,128]{2,1,0:T(8,128)(2,1)S(1)} custom-call(s32[8]{0:T(128)S(1)} %compare_select_fusion.6.place, bf16[2,12,24,128]{3,2,1,0:T(8,128)(2,1)S(1)} %get-tuple-element.37.refs_0_, bf16[2,12,24,128]{3,2,1,0:T(8,128)(2,1)S(1)} %get-tuple-element.38.refs_1_, bf16[2,12,24,128]{3,2,1,0:T(8,128)(2,1)S(1)} %get-tuple-element.39.refs_2_, ...), custom_call_target="tpu_custom_call" | custom-call | flops 2000000000 | bytes 1327104 | tf_op jit(solution)/shard_map/pallas_call | solution.py:42
  41.8 3.1 %collective-permute-start.16 = (bf16[12,48,128]{2,1,0:T(8,128)(2,1)S(1)}, bf16[12,48,128]{2,1,0:T(8,128)(2,1)S(1)}, u32[]{:S(2)}, u32[]{:S(2)}) collective-permute-start(bf16[12,48,128]{2,1,0:T(8,128)(2,1)S(1)} %shard_map.87), channel_id=1, source_target_pairs={{0,8},{2,10},{4,12},{6,14},{8,0},{10,2},{12,4},{14,6},{1,9},{3,11}... | collective-permute-start | bytes 442376 | tf_op jit(solution)/shard_map/ppermute | solution.py:244
  44.9 1.2 %shard_map.88 = bf16[12,48,128]{2,1,0:T(8,128)(2,1)S(1)} custom-call(s32[8]{0:T(128)S(1)} %compare_select_fusion.6.place, bf16[2,12,24,128]{3,2,1,0:T(8,128)(2,1)S(1)} %get-tuple-element.37.refs_0_, bf16[2,12,24,128]{3,2,1,0:T(8,128)(2,1)S(1)} %get-tuple-element.38.refs_1_, bf16[2,12,24,128]{3,2,1,0:T(8,128)(2,1)S(1)} %get-tuple-element.39.refs_2_, ...), custom_call_target="tpu_custom_call" | custom-call | flops 2000000000 | bytes 1327104 | tf_op jit(solution)/shard_map/pallas_call | solution.py:42
  46.1 0.0 copy-start.1
  46.1 0.0 copy-start.3
  46.1 1.4 %collective-permute-start.17 = (bf16[12,48,128]{2,1,0:T(8,128)(2,1)S(1)}, bf16[12,48,128]{2,1,0:T(8,128)(2,1)S(1)}, u32[]{:S(2)}, u32[]{:S(2)}) collective-permute-start(bf16[12,48,128]{2,1,0:T(8,128)(2,1)S(1)} %shard_map.88), channel_id=1, source_target_pairs={{0,12},{2,14},{4,8},{6,10},{8,4},{10,6},{12,0},{14,2},{1,13},{3,15... | collective-permute-start | bytes 442376 | tf_op jit(solution)/shard_map/ppermute | solution.py:244
  47.5 1.2 %shard_map.85.own = f32[12,48,128]{2,1,0:T(8,128)S(1)} custom-call(s32[8]{0:T(128)S(1)} %compare_select_fusion.6.place, bf16[2,12,24,128]{3,2,1,0:T(8,128)(2,1)S(1)} %get-tuple-element.37.refs_0_, bf16[2,12,24,128]{3,2,1,0:T(8,128)(2,1)S(1)} %get-tuple-element.38.refs_1_, bf16[2,12,24,128]{3,2,1,0:T(8,128)(2,1)S(1)} %get-tuple-element.39.refs_2_, ...), custom_call_target="tpu_custom_call" | custom-call | flops 2000000000 | bytes 1474560 | tf_op jit(solution)/shard_map/pallas_call | solution.py:42
  48.7 7.3 %collective-permute-done.16.refs_1_ = bf16[12,48,128]{2,1,0:T(8,128)(2,1)S(1)} collective-permute-done((bf16[12,48,128]{2,1,0:T(8,128)(2,1)S(1)}, bf16[12,48,128]{2,1,0:T(8,128)(2,1)S(1)}, u32[]{:S(2)}, u32[]{:S(2)}) %collective-permute-start.16) | collective-permute-done | bytes 147488 | tf_op jit(solution)/shard_map/ppermute | solution.py:244
  56.0 2.4 %shard_map.89 = bf16[12,48,128]{2,1,0:T(8,128)(2,1)} custom-call(s32[8]{0:T(128)S(1)} %compare_select_fusion.6.place, bf16[12,48,128]{2,1,0:T(8,128)(2,1)S(1)} %get-tuple-element.35.stream, f32[576,128]{1,0:T(8,128)S(1)} %get-tuple-element.36.gate, bf16[2,128,128]{2,1,0:T(8,128)(2,1)S(1)} %copy-done.5, bf16[128,1024]{1,0:T(8,128)(2,1)S(1)} %copy-done.1, ...), custom_call_target="tpu_custom_call" | custom-call | flops 2000000000 | bytes 1785856 | tf_op jit(solution)/shard_map/pallas_call | solution.py:42
  (18 shorter events, 0.0 us)
Async XLA Ops:
  0.7 7.7 %copy-start.2 = (bf16[12,48,128]{2,1,0:T(8,128)(2,1)S(1)}, bf16[12,48,128]{2,1,0:T(8,128)(2,1)}, u32[]{:S(2)}) copy-start(bf16[12,48,128]{2,1,0:T(8,128)(2,1)} %pair.3) | copy-start | bytes 442372
  0.7 9.4 %copy-start = (bf16[2,128,512]{2,1,0:T(8,128)(2,1)S(1)}, bf16[2,128,512]{2,1,0:T(8,128)(2,1)}, u32[]{:S(2)}) copy-start(bf16[2,128,512]{2,1,0:T(8,128)(2,1)} %weight_in.7) | copy-start | bytes 786436
  2.6 9.9 %collective-permute-start.8 = (bf16[12,48,128]{2,1,0:T(8,128)(2,1)S(1)}, bf16[12,48,128]{2,1,0:T(8,128)(2,1)S(1)}, u32[]{:S(2)}, u32[]{:S(2)}) collective-permute-start(bf16[12,48,128]{2,1,0:T(8,128)(2,1)S(1)} %shard_map.75.b_same), channel_id=1, source_target_pairs={{0,12},{2,14},{4,8},{6,10},{8,4},{10,6},{12,0},{14,2},{1,13},{3,15... | collective-permute-start | bytes 442376 | tf_op jit(solution)/shard_map/ppermute | solution.py:244
  7.8 12.5 %collective-permute-start.5 = (bf16[12,48,128]{2,1,0:T(8,128)(2,1)S(1)}, bf16[12,48,128]{2,1,0:T(8,128)(2,1)S(1)}, u32[]{:S(2)}, u32[]{:S(2)}) collective-permute-start(bf16[12,48,128]{2,1,0:T(8,128)(2,1)S(1)} %shard_map.75.b_same), channel_id=1, source_target_pairs={{0,8},{2,10},{4,12},{6,14},{8,0},{10,2},{12,4},{14,6},{1,9},{3,11}... | collective-permute-start | bytes 442376 | tf_op jit(solution)/shard_map/ppermute | solution.py:244
  7.8 12.5 %collective-permute-start.2 = (bf16[12,48,128]{2,1,0:T(8,128)(2,1)S(1)}, bf16[12,48,128]{2,1,0:T(8,128)(2,1)S(1)}, u32[]{:S(2)}, u32[]{:S(2)}) collective-permute-start(bf16[12,48,128]{2,1,0:T(8,128)(2,1)S(1)} %shard_map.75.b_same), channel_id=1, source_target_pairs={{0,4},{2,6},{4,0},{6,2},{8,12},{10,14},{12,8},{14,10},{1,5},{3,7},... | collective-permute-start | bytes 442376 | tf_op jit(solution)/shard_map/ppermute | solution.py:244
  8.4 12.4 %collective-permute-start.1 = (bf16[12,48,128]{2,1,0:T(8,128)(2,1)S(1)}, bf16[12,48,128]{2,1,0:T(8,128)(2,1)S(1)}, u32[]{:S(2)}, u32[]{:S(2)}) collective-permute-start(bf16[12,48,128]{2,1,0:T(8,128)(2,1)S(1)} %shard_map.75.b_same), channel_id=1, source_target_pairs={{0,2},{2,0},{4,6},{6,4},{8,10},{10,8},{12,14},{14,12},{1,3},{3,1},... | collective-permute-start | bytes 442376 | tf_op jit(solution)/shard_map/ppermute | solution.py:244
  8.4 13.7 %collective-permute-start = (bf16[12,48,128]{2,1,0:T(8,128)(2,1)S(1)}, bf16[12,48,128]{2,1,0:T(8,128)(2,1)S(1)}, u32[]{:S(2)}, u32[]{:S(2)}) collective-permute-start(bf16[12,48,128]{2,1,0:T(8,128)(2,1)S(1)} %copy-done.2), channel_id=1, source_target_pairs={{0,1},{1,0},{2,3},{3,2},{4,5},{5,4},{6,7},{7,6},{8,9},{9,8},{10,11... | collective-permute-start | bytes 442376 | tf_op jit(solution)/shard_map/ppermute | solution.py:247
  11.0 11.1 %copy-start.4 = (bf16[2,128,128]{2,1,0:T(8,128)(2,1)S(1)}, bf16[2,128,128]{2,1,0:T(8,128)(2,1)}, u32[]{:S(2)}) copy-start(bf16[2,128,128]{2,1,0:T(8,128)(2,1)} %weight_gate.3) | copy-start | bytes 196612
  12.6 10.6 %collective-permute-start.9 = (bf16[12,48,128]{2,1,0:T(8,128)(2,1)S(1)}, bf16[12,48,128]{2,1,0:T(8,128)(2,1)S(1)}, u32[]{:S(2)}, u32[]{:S(2)}) collective-permute-start(bf16[12,48,128]{2,1,0:T(8,128)(2,1)S(1)} %collective-permute-done.8.b_same), channel_id=1, source_target_pairs={{0,2},{2,0},{4,6},{6,4},{8,10},{10,8},{12,14},{14,12},{1,3},{3,1},... | collective-permute-start | bytes 442376 | tf_op jit(solution)/shard_map/ppermute | solution.py:244
  20.2 5.9 %collective-permute-start.6 = (bf16[12,48,128]{2,1,0:T(8,128)(2,1)S(1)}, bf16[12,48,128]{2,1,0:T(8,128)(2,1)S(1)}, u32[]{:S(2)}, u32[]{:S(2)}) collective-permute-start(bf16[12,48,128]{2,1,0:T(8,128)(2,1)S(1)} %collective-permute-done.5.b_same), channel_id=1, source_target_pairs={{0,2},{2,0},{4,6},{6,4},{8,10},{10,8},{12,14},{14,12},{1,3},{3,1},... | collective-permute-start | bytes 442376 | tf_op jit(solution)/shard_map/ppermute | solution.py:244
  20.2 7.8 %collective-permute-start.3 = (bf16[12,48,128]{2,1,0:T(8,128)(2,1)S(1)}, bf16[12,48,128]{2,1,0:T(8,128)(2,1)S(1)}, u32[]{:S(2)}, u32[]{:S(2)}) collective-permute-start(bf16[12,48,128]{2,1,0:T(8,128)(2,1)S(1)} %collective-permute-done.2.b_same), channel_id=1, source_target_pairs={{0,2},{2,0},{4,6},{6,4},{8,10},{10,8},{12,14},{14,12},{1,3},{3,1},... | collective-permute-start | bytes 442376 | tf_op jit(solution)/shard_map/ppermute | solution.py:244
  24.5 9.0 %collective-permute-start.10 = (bf16[288,128]{1,0:T(8,128)(2,1)S(1)}, bf16[288,128]{1,0:T(8,128)(2,1)S(1)}, u32[]{:S(2)}, u32[]{:S(2)}) collective-permute-start(bf16[288,128]{1,0:T(8,128)(2,1)S(1)} %get-tuple-element.33), channel_id=1, source_target_pairs={{0,1},{1,0},{2,3},{3,2},{4,5},{5,4},{6,7},{7,6},{8,9},{9,8},{10,11... | collective-permute-start | bytes 221192 | tf_op jit(solution)/shard_map/ppermute | solution.py:247
  27.4 4.8 %copy-start.5 = (bf16[2,128,128]{2,1,0:T(8,128)(2,1)S(1)}, bf16[2,128,128]{2,1,0:T(8,128)(2,1)}, u32[]{:S(2)}) copy-start(bf16[2,128,128]{2,1,0:T(8,128)(2,1)} %weight_out.9) | copy-start | bytes 196612
  27.5 4.8 %collective-permute-start.7 = (bf16[288,128]{1,0:T(8,128)(2,1)S(1)}, bf16[288,128]{1,0:T(8,128)(2,1)S(1)}, u32[]{:S(2)}, u32[]{:S(2)}) collective-permute-start(bf16[288,128]{1,0:T(8,128)(2,1)S(1)} %get-tuple-element.30), channel_id=1, source_target_pairs={{0,1},{1,0},{2,3},{3,2},{4,5},{5,4},{6,7},{7,6},{8,9},{9,8},{10,11... | collective-permute-start | bytes 221192 | tf_op jit(solution)/shard_map/ppermute | solution.py:247
  29.4 5.9 %collective-permute-start.4 = (bf16[576,128]{1,0:T(8,128)(2,1)S(1)}, bf16[576,128]{1,0:T(8,128)(2,1)S(1)}, u32[]{:S(2)}, u32[]{:S(2)}) collective-permute-start(bf16[576,128]{1,0:T(8,128)(2,1)S(1)} %get-tuple-element.25), channel_id=1, source_target_pairs={{0,1},{1,0},{2,3},{3,2},{4,5},{5,4},{6,7},{7,6},{8,9},{9,8},{10,11... | collective-permute-start | bytes 442376 | tf_op jit(solution)/shard_map/ppermute | solution.py:247
  33.5 5.9 %collective-permute-start.13 = (bf16[2,12,24,128]{3,2,1,0:T(8,128)(2,1)S(1)}, bf16[2,12,24,128]{3,2,1,0:T(8,128)(2,1)S(1)}, u32[]{:S(2)}, u32[]{:S(2)}) collective-permute-start(bf16[2,12,24,128]{3,2,1,0:T(8,128)(2,1)S(1)} %get-tuple-element.39.refs_2_), channel_id=1, source_target_pairs={{0,2},{2,0},{4,6},{6,4},{8,10},{10,8},{12,14},{14,12},{1,3},{3,1},... | collective-permute-start | bytes 442376 | tf_op jit(solution)/shard_map/ppermute | solution.py:244
  34.8 4.6 %collective-permute-start.14 = (bf16[2,12,24,128]{3,2,1,0:T(8,128)(2,1)S(1)}, bf16[2,12,24,128]{3,2,1,0:T(8,128)(2,1)S(1)}, u32[]{:S(2)}, u32[]{:S(2)}) collective-permute-start(bf16[2,12,24,128]{3,2,1,0:T(8,128)(2,1)S(1)} %get-tuple-element.40.refs_3_), channel_id=1, source_target_pairs={{0,2},{2,0},{4,6},{6,4},{8,10},{10,8},{12,14},{14,12},{1,3},{3,1},... | collective-permute-start | bytes 442376 | tf_op jit(solution)/shard_map/ppermute | solution.py:244
  36.6 2.8 %collective-permute-start.12 = (bf16[2,12,24,128]{3,2,1,0:T(8,128)(2,1)S(1)}, bf16[2,12,24,128]{3,2,1,0:T(8,128)(2,1)S(1)}, u32[]{:S(2)}, u32[]{:S(2)}) collective-permute-start(bf16[2,12,24,128]{3,2,1,0:T(8,128)(2,1)S(1)} %get-tuple-element.38.refs_1_), channel_id=1, source_target_pairs={{0,2},{2,0},{4,6},{6,4},{8,10},{10,8},{12,14},{14,12},{1,3},{3,1},... | collective-permute-start | bytes 442376 | tf_op jit(solution)/shard_map/ppermute | solution.py:244
  37.9 1.6 %collective-permute-start.11 = (bf16[2,12,24,128]{3,2,1,0:T(8,128)(2,1)S(1)}, bf16[2,12,24,128]{3,2,1,0:T(8,128)(2,1)S(1)}, u32[]{:S(2)}, u32[]{:S(2)}) collective-permute-start(bf16[2,12,24,128]{3,2,1,0:T(8,128)(2,1)S(1)} %get-tuple-element.37.refs_0_), channel_id=1, source_target_pairs={{0,2},{2,0},{4,6},{6,4},{8,10},{10,8},{12,14},{14,12},{1,3},{3,1},... | collective-permute-start | bytes 442376 | tf_op jit(solution)/shard_map/ppermute | solution.py:244
  40.6 8.1 %collective-permute-start.15 = (bf16[12,48,128]{2,1,0:T(8,128)(2,1)S(1)}, bf16[12,48,128]{2,1,0:T(8,128)(2,1)S(1)}, u32[]{:S(2)}, u32[]{:S(2)}) collective-permute-start(bf16[12,48,128]{2,1,0:T(8,128)(2,1)S(1)} %shard_map.86), channel_id=1, source_target_pairs={{0,4},{2,6},{4,0},{6,2},{8,12},{10,14},{12,8},{14,10},{1,5},{3,7},... | collective-permute-start | bytes 442376 | tf_op jit(solution)/shard_map/ppermute | solution.py:244
  41.8 14.2 %collective-permute-start.16 = (bf16[12,48,128]{2,1,0:T(8,128)(2,1)S(1)}, bf16[12,48,128]{2,1,0:T(8,128)(2,1)S(1)}, u32[]{:S(2)}, u32[]{:S(2)}) collective-permute-start(bf16[12,48,128]{2,1,0:T(8,128)(2,1)S(1)} %shard_map.87), channel_id=1, source_target_pairs={{0,8},{2,10},{4,12},{6,14},{8,0},{10,2},{12,4},{14,6},{1,9},{3,11}... | collective-permute-start | bytes 442376 | tf_op jit(solution)/shard_map/ppermute | solution.py:244
  46.1 9.9 %copy-start.1 = (bf16[128,1024]{1,0:T(8,128)(2,1)S(1)}, bf16[128,1024]{1,0:T(8,128)(2,1)}, u32[]{:S(2)}) copy-start(bf16[128,1024]{1,0:T(8,128)(2,1)} %trans_in.1) | copy-start | bytes 786436
  46.1 9.9 %copy-start.3 = (bf16[512,128]{1,0:T(8,128)(2,1)S(1)}, bf16[512,128]{1,0:T(8,128)(2,1)}, u32[]{:S(2)}) copy-start(bf16[512,128]{1,0:T(8,128)(2,1)} %trans_out.1) | copy-start | bytes 393220
  46.1 9.9 %collective-permute-start.17 = (bf16[12,48,128]{2,1,0:T(8,128)(2,1)S(1)}, bf16[12,48,128]{2,1,0:T(8,128)(2,1)S(1)}, u32[]{:S(2)}, u32[]{:S(2)}) collective-permute-start(bf16[12,48,128]{2,1,0:T(8,128)(2,1)S(1)} %shard_map.88), channel_id=1, source_target_pairs={{0,12},{2,14},{4,8},{6,10},{8,4},{10,6},{12,0},{14,2},{1,13},{3,15... | collective-permute-start | bytes 442376 | tf_op jit(solution)/shard_map/ppermute | solution.py:244

commit v2 on v1

--- a/solution.py
+++ b/solution.py
@@ -24,11 +24,35 @@
     return jnp.dot(left, right, preferred_element_type=F32)
 
 
-def keep_of(place, rows, cols, width):
-    shape = (rows, cols, width)
-    row = lax.broadcasted_iota(jnp.int32, shape, 0) + place[0]
-    col = lax.broadcasted_iota(jnp.int32, shape, 1) + place[1]
-    return jnp.where((row < place[2]) & (col < place[2]), 1.0, 0.0).astype(F32)
+class Place:
+
+    def __init__(self, n_row, n_col, limit=None):
+        self.n_row, self.n_col, self.limit = n_row, n_col, limit
+        self.per = n_row // 2 // n_col
+
+    def row(self):
+        return lax.axis_index("row")
+
+    def col(self):
+        return lax.axis_index("col")
+
+    def core(self):
+        return lax.rem(self.row(), 2)
+
+    def chip(self):
+        return lax.div(self.row(), 2)
+
+    def group(self):
+        return lax.div(self.chip(), self.per) ^ self.col()
+
+    def piece(self):
+        return lax.rem(self.chip(), self.per)
+
+    def keep(self, first_row, first_col, shape):
+        row = lax.broadcasted_iota(jnp.int32, shape, 0) + first_row
+        col = lax.broadcasted_iota(jnp.int32, shape, 1) + first_col
+        count = self.limit[:1, : shape[2]].reshape(1, 1, shape[2])
+        return jnp.where((row < count) & (col < count), 1.0, 0.0).astype(F32)
 
 
 def gated(normed, weight, side, which, hidden):
@@ -37,18 +61,27 @@
     return jax.nn.sigmoid(gate) * value
 
 
-def call(kernel, outs, *args, scratch=(), flops=2_000_000_000, space=pltpu.VMEM):
-    nbytes = sum(a.size * a.dtype.itemsize for a in (*args[1:], *outs))
-    return pl.pallas_call(
-        kernel,
+def call(kernel, outs, place, *args, scratch=(), flops=2_000_000_000, space=pltpu.VMEM, masked=False):
+    nbytes = sum(a.size * a.dtype.itemsize for a in (*args, *outs))
+
+    def run(*refs):
+        if masked:
+            kernel(Place(place.n_row, place.n_col, refs[0]), *refs[1:])
+        else:
+            kernel(place, *refs)
+
+    limit = [place.limit] if masked else []
+    run = pl.pallas_call(
+        run,
         out_shape=outs,
-        in_specs=[pl.BlockSpec(memory_space=pltpu.SMEM)]
-        + [pl.BlockSpec(memory_space=space)] * (len(args) - 1),
+        in_specs=[pl.BlockSpec(memory_space=pltpu.VMEM)] * len(limit)
+        + [pl.BlockSpec(memory_space=space)] * len(args),
         out_specs=[pl.BlockSpec(memory_space=pltpu.VMEM)] * len(outs),
         scratch_shapes=scratch,
         cost_estimate=pl.CostEstimate(flops=flops, bytes_accessed=nbytes, transcendentals=0),
         compiler_params=pltpu.CompilerParams(vmem_limit_bytes=VMEM_LIMIT),
-    )(*args)
+    )
+    return run(*limit, *args)
 
 
 def start_kernel(place, pair, weight, b_out, tile, value, gate, sems):
@@ -70,7 +103,7 @@
         copy.wait()
     normed = norm(tile[...].astype(F32)).astype(BF16).reshape(rows * cols, width)
     b = (jax.nn.sigmoid(dot(normed, gate[...])) * dot(normed, value[...])).reshape(rows, cols, hidden)
-    b_out[...] = (keep_of(place, rows, cols, hidden) * b).astype(BF16)
+    b_out[...] = (place.keep(place.row() * rows, place.col() * cols, (rows, cols, hidden)) * b).astype(BF16)
 
 
 def second_kernel(place, pair, weight, a_out):
@@ -78,7 +111,7 @@
     hidden = a_out.shape[2]
     normed = norm(pair[...].astype(F32)).astype(BF16).reshape(rows * cols, width)
     a = gated(normed, weight, 0, 0, hidden).reshape(rows, cols, hidden)
-    a_out[...] = (keep_of(place, rows, cols, hidden) * a).astype(BF16).astype(F32)
+    a_out[...] = (place.keep(place.row() * rows, place.col() * cols, (rows, cols, hidden)) * a).astype(BF16).astype(F32)
 
 
 def gates_kernel(place, weight_gate, *refs):
@@ -100,7 +133,7 @@
     step = 2 if rows % 2 == 0 else 1
     for swap, block in enumerate((b_same, b_other)):
         wide[...] = block[...].astype(F32)
-        first = rows * (place[3] ^ swap)
+        first = rows * (place.core() ^ swap)
 
         @pl.loop(0, rows // step)
         def _(turn):
@@ -124,13 +157,11 @@
     for other in others:
         total = total + other[which_cut * rows * span : (which_cut + 1) * rows * span].astype(F32)
     group, piece = divmod(step, per)
-    which = (place[4] ^ group) * per + (place[5] ^ piece)
+    which = (place.group() ^ group) * per + (place.piece() ^ piece)
     mixnorm = norm(total).astype(BF16)
     update = gates[which] * dot(mixnorm, weight_out[0])
     shape = (rows, span, width)
-    row = lax.broadcasted_iota(jnp.int32, shape, 0) + place[0]
-    col = lax.broadcasted_iota(jnp.int32, shape, 1) + (place[6] ^ step) * span
-    keep = jnp.where((row < place[2]) & (col < place[2]), 1.0, 0.0).astype(F32).reshape(rows * span, width)
+    keep = place.keep(place.row() * rows, (place.chip() ^ step) * span, shape).reshape(rows * span, width)
     stream = (pairs[which] + keep * update).astype(BF16)
     stream_out[...] = stream
     normed = norm(stream.astype(F32)).astype(BF16)
@@ -147,16 +178,16 @@
         wide_a[half * rows : (half + 1) * rows] = source[0].astype(F32)
     for group in range(len(same) // per):
 
-        @pl.when(place[4] == group)
+        @pl.when(place.group() == group)
         def _():
             for piece in range(per):
-                first = pl.multiple_of((place[5] ^ piece) * span, 8)
+                first = pl.multiple_of((place.piece() ^ piece) * span, 8)
                 for half, source in enumerate((same, other)):
                     value = source[group * per + piece][1].astype(F32)
                     wide_b[half * rows : (half + 1) * rows, pl.ds(first, span), :] = value
 
     steps = 4 if rows % 4 == 0 else 1
-    first = place[3] * rows
+    first = place.core() * rows
 
     @pl.loop(0, rows // steps)
     def _(turn):
@@ -177,10 +208,10 @@
     span = 2 * rows
     for group in range(len(pieces) // per):
 
-        @pl.when(place[4] == group)
+        @pl.when(place.group() == group)
         def _():
             for piece in range(per):
-                first = pl.multiple_of((place[5] ^ piece) * span, 8)
+                first = pl.multiple_of((place.piece() ^ piece) * span, 8)
                 value = pieces[group * per + piece][...].astype(F32).reshape(rows, span, width)
                 wide[:, pl.ds(first, span), :] = value
 
@@ -199,7 +230,7 @@
     hidden = total.shape[2]
     mixnorm = norm(total.reshape(rows * cols, hidden)).astype(BF16)
     update = (gate[...] * dot(mixnorm, weight_out[1])).reshape(rows, cols, width)
-    keep = keep_of(place, rows, cols, width)
+    keep = place.keep(place.row() * rows, place.col() * cols, (rows, cols, width))
     after = (stream[...].astype(F32) + keep * update).astype(BF16)
     normed = norm(after.astype(F32)).astype(BF16).reshape(rows * cols, width)
     ffn = trans_out.shape[0]
@@ -223,22 +254,8 @@
     n_chip = n_row // 2
     per = n_chip // n_col
     span = 2 * rows
-    row_place = lax.axis_index("row")
-    col_place = lax.axis_index("col")
-    chip = row_place // 2
-    lane = jnp.arange(8, dtype=jnp.int32)
-    values = (
-        row_place * rows,
-        col_place * cols,
-        token_count[0],
-        row_place % 2,
-        (chip // per) ^ col_place,
-        chip % per,
-        chip,
-    )
-    place = jnp.zeros((8,), jnp.int32)
-    for where, value in enumerate(values):
-        place = jnp.where(lane == where, value, place)
+    limit = jnp.broadcast_to(token_count.reshape(1, 1), (8, max(width, hidden)))
+    place = Place(n_row, n_col, limit)
 
     def along_row(value, mask):
         return lax.ppermute(value, "row", [(i, i ^ mask) for i in range(n_row)])
@@ -265,12 +282,13 @@
             pltpu.SemaphoreType.DMA((3,)),
         ],
         space=pltpu.HBM,
+        masked=True,
     )
     turns = sequence(n_chip)
     arrived = {0: b}
     for step in turns[1:]:
         arrived[step] = along_row(b, 2 * step)
-    (a,) = call(second_kernel, [shape(*tile, dtype=F32)], place, pair, tri_in)
+    (a,) = call(second_kernel, [shape(*tile, dtype=F32)], place, pair, tri_in, masked=True)
     pairs, gates = call(gates_kernel, [shape(n_chip, *cut, dtype=F32)] * 2, place, tri_gate, *tiles)
     streams, same, other = ({}, {}, {})
     parts = {}
@@ -302,6 +320,7 @@
                 tri_in,
                 parts[ready],
                 *sent,
+                masked=True,
             )
             other[ready] = along_row(same[ready], 1)
     totals = {}
@@ -334,6 +353,7 @@
         trans_in,
         trans_out,
         *[totals[step] for step in range(n_chip)],
+        masked=True,
     )
     return out
 

time: 58.7 us -> 53 us (0.903)
  Pallas kernels: 22.2 us -> 13 us
  waiting for transfers between devices: 17.8 us -> 21.3 us
    pallas_call x17, Pallas kernels: 22.2 us -> 13 us  [call(): return run(*limit, *args)]
    ppermute x14, waiting for transfers between devices: 16.6 us -> 18.8 us  [along_row(): return lax.ppermute(value, 'row', [(i, i ^ mask) for i in range(n_row)])]
    ppermute x4, waiting for transfers between devices: 1.27 us -> 2.5 us  [along_col(): return lax.ppermute(value, 'col', [(i, i ^ mask) for i in range(n_col)])]
  transfers between devices with their start and end apart: 18 -> 18, of which waited for: 4 -> 7; matrix products, arithmetic and copies ran while one was open for 0% -> 0% of each run, Pallas kernels for 29% -> 17%
where the time goes in v2:
time: 53 us; the launch traced here: 52.7 us
  waiting for transfers between devices  21.3 us (40%)
  starting transfers between devices  17.5 us (33%)
  Pallas kernels  13 us (25%)
  between operations  0.88 us (2%)
    ppermute x14, waiting for transfers between devices, along_row(): return lax.ppermute(value, 'row', [(i, i ^ mask) for i in range(n_row)])  18.8 us
    pallas_call x17, Pallas kernels, call(): return run(*limit, *args)  13 us
    ppermute x14, starting transfers between devices, along_row(): return lax.ppermute(value, 'row', [(i, i ^ mask) for i in range(n_row)])  12.1 us
    ppermute x4, starting transfers between devices, along_col(): return lax.ppermute(value, 'col', [(i, i ^ mask) for i in range(n_col)])  5.35 us
    ppermute x4, waiting for transfers between devices, along_col(): return lax.ppermute(value, 'col', [(i, i ^ mask) for i in range(n_col)])  2.5 us
  transfers between devices with their start and end apart: 18, of which 7 were waited for; matrix products, arithmetic and copies ran while one was open for 0% of the time, Pallas kernels for 17%

profile of v2, /device:TPU:0, one launch (start us, length us, event | category | flops | bytes accessed | tf_op | source)
XLA Modules:
  0.0 52.7 jit_solution(13941332553235740760)
XLA Ops:
  0.7 0.0 copy-start.2
  0.7 0.0 copy-start
  0.7 1.4 %shard_map.75.refs_1_ = bf16[12,48,128]{2,1,0:T(8,128)(2,1)S(1)} custom-call(s32[8,128]{1,0:T(8,128)S(1)} %broadcast_in_dim.8.refs_0_, bf16[12,48,128]{2,1,0:T(8,128)(2,1)} %refs_1_.5, bf16[2,128,512]{2,1,0:T(8,128)(2,1)} %refs_4_.8), custom_call_target="tpu_custom_call" | custom-call | flops 2000000000 | bytes 557056 | tf_op jit(solution)/shard_map/pallas_call | solution.py:84
  2.1 5.1 %collective-permute-start.8 = (bf16[12,48,128]{2,1,0:T(8,128)(2,1)S(1)}, bf16[12,48,128]{2,1,0:T(8,128)(2,1)S(1)}, u32[]{:S(2)}, u32[]{:S(2)}) collective-permute-start(bf16[12,48,128]{2,1,0:T(8,128)(2,1)S(1)} %shard_map.75.refs_1_), channel_id=1, source_target_pairs={{0,12},{2,14},{4,8},{6,10},{8,4},{10,6},{12,0},{14,2},{1,13},{3,15... | collective-permute-start | bytes 442376 | tf_op jit(solution)/shard_map/ppermute | solution.py:261
  7.3 0.0 collective-permute-start.5
  7.3 0.6 %collective-permute-start.2 = (bf16[12,48,128]{2,1,0:T(8,128)(2,1)S(1)}, bf16[12,48,128]{2,1,0:T(8,128)(2,1)S(1)}, u32[]{:S(2)}, u32[]{:S(2)}) collective-permute-start(bf16[12,48,128]{2,1,0:T(8,128)(2,1)S(1)} %shard_map.75.refs_1_), channel_id=1, source_target_pairs={{0,4},{2,6},{4,0},{6,2},{8,12},{10,14},{12,8},{14,10},{1,5},{3,7},... | collective-permute-start | bytes 442376 | tf_op jit(solution)/shard_map/ppermute | solution.py:261
  7.9 0.0 collective-permute-start.1
  7.9 1.6 %collective-permute-start = (bf16[12,48,128]{2,1,0:T(8,128)(2,1)S(1)}, bf16[12,48,128]{2,1,0:T(8,128)(2,1)S(1)}, u32[]{:S(2)}, u32[]{:S(2)}) collective-permute-start(bf16[12,48,128]{2,1,0:T(8,128)(2,1)S(1)} %copy-done.2), channel_id=1, source_target_pairs={{0,1},{1,0},{2,3},{3,2},{4,5},{5,4},{6,7},{7,6},{8,9},{9,8},{10,11... | collective-permute-start | bytes 442376 | tf_op jit(solution)/shard_map/ppermute | solution.py:264
  9.5 0.4 shard_map.74.refs_0_
  10.0 0.0 copy-start.4
  10.0 2.1 %collective-permute-done.8.refs_1_ = bf16[12,48,128]{2,1,0:T(8,128)(2,1)S(1)} collective-permute-done((bf16[12,48,128]{2,1,0:T(8,128)(2,1)S(1)}, bf16[12,48,128]{2,1,0:T(8,128)(2,1)S(1)}, u32[]{:S(2)}, u32[]{:S(2)}) %collective-permute-start.8) | collective-permute-done | bytes 147488 | tf_op jit(solution)/shard_map/ppermute | solution.py:261
  12.1 0.0 collective-permute-start.9
  12.1 7.7 %collective-permute-done.5.refs_1_ = bf16[12,48,128]{2,1,0:T(8,128)(2,1)S(1)} collective-permute-done((bf16[12,48,128]{2,1,0:T(8,128)(2,1)S(1)}, bf16[12,48,128]{2,1,0:T(8,128)(2,1)S(1)}, u32[]{:S(2)}, u32[]{:S(2)}) %collective-permute-start.5) | collective-permute-done | bytes 147488 | tf_op jit(solution)/shard_map/ppermute | solution.py:261
  19.7 0.0 collective-permute-start.6
  19.7 0.5 collective-permute-start.3
  20.3 0.8 %shard_map.76.refs_3_.refs_5_ = f32[12,24,128]{2,1,0:T(8,128)S(1)} custom-call(f32[12,48,128]{2,1,0:T(8,128)S(1)} %shard_map.74.refs_0_, bf16[12,48,128]{2,1,0:T(8,128)(2,1)S(1)} %shard_map.75.refs_1_, bf16[12,48,128]{2,1,0:T(8,128)(2,1)S(1)} %collective-permute-done.1.refs_2_), custom_call_target="tpu_custom_call" | custom-call | flops 2000000000 | bytes 737280 | tf_op jit(solution)/shard_map/pallas_call | solution.py:84
  21.1 0.5 shard_map.73
  21.6 0.8 %shard_map.82 = (f32[12,24,128]{2,1,0:T(8,128)S(1)}, bf16[288,128]{1,0:T(8,128)(2,1)S(1)}) custom-call(f32[12,48,128]{2,1,0:T(8,128)S(1)} %shard_map.74.refs_0_, bf16[12,48,128]{2,1,0:T(8,128)(2,1)S(1)} %collective-permute-done.8.refs_1_, bf16[12,48,128]{2,1,0:T(8,128)(2,1)S(1)} %collective-permute-done.9.refs_2_), custom_call_target="tpu_custom_call" | custom-call | flops 2000000000 | bytes 811008 | tf_op jit(solution)/shard_map/pallas_call | solution.py:84
  22.4 1.6 %collective-permute-start.10 = (bf16[288,128]{1,0:T(8,128)(2,1)S(1)}, bf16[288,128]{1,0:T(8,128)(2,1)S(1)}, u32[]{:S(2)}, u32[]{:S(2)}) collective-permute-start(bf16[288,128]{1,0:T(8,128)(2,1)S(1)} %get-tuple-element.33), channel_id=1, source_target_pairs={{0,1},{1,0},{2,3},{3,2},{4,5},{5,4},{6,7},{7,6},{8,9},{9,8},{10,11... | collective-permute-start | bytes 221192 | tf_op jit(solution)/shard_map/ppermute | solution.py:264
  24.0 0.8 %shard_map.80 = (f32[12,24,128]{2,1,0:T(8,128)S(1)}, bf16[288,128]{1,0:T(8,128)(2,1)S(1)}) custom-call(f32[12,48,128]{2,1,0:T(8,128)S(1)} %shard_map.74.refs_0_, bf16[12,48,128]{2,1,0:T(8,128)(2,1)S(1)} %collective-permute-done.5.refs_1_, bf16[12,48,128]{2,1,0:T(8,128)(2,1)S(1)} %collective-permute-done.6.refs_2_), custom_call_target="tpu_custom_call" | custom-call | flops 2000000000 | bytes 811008 | tf_op jit(solution)/shard_map/pallas_call | solution.py:84
  24.8 0.0 copy-start.5
  24.8 0.6 %collective-permute-start.7 = (bf16[288,128]{1,0:T(8,128)(2,1)S(1)}, bf16[288,128]{1,0:T(8,128)(2,1)S(1)}, u32[]{:S(2)}, u32[]{:S(2)}) collective-permute-start(bf16[288,128]{1,0:T(8,128)(2,1)S(1)} %get-tuple-element.30), channel_id=1, source_target_pairs={{0,1},{1,0},{2,3},{3,2},{4,5},{5,4},{6,7},{7,6},{8,9},{9,8},{10,11... | collective-permute-start | bytes 221192 | tf_op jit(solution)/shard_map/ppermute | solution.py:264
  25.4 0.8 %shard_map.77 = (f32[12,24,128]{2,1,0:T(8,128)S(1)}, bf16[576,128]{1,0:T(8,128)(2,1)S(1)}) custom-call(f32[12,48,128]{2,1,0:T(8,128)S(1)} %shard_map.74.refs_0_, bf16[12,48,128]{2,1,0:T(8,128)(2,1)S(1)} %collective-permute-done.2.refs_1_, bf16[12,48,128]{2,1,0:T(8,128)(2,1)S(1)} %collective-permute-done.3.refs_2_, f32[12,24,128]{2,1,0:T(8,128)S(1)} %shard_map.76.refs_3_.refs_5_), custom_call_target="tpu_custom_call" | custom-call | flops 2000000000 | bytes 1032192 | tf_op jit(solution)/shard_map/pallas_call | solution.py:84
  26.2 1.6 %collective-permute-start.4 = (bf16[576,128]{1,0:T(8,128)(2,1)S(1)}, bf16[576,128]{1,0:T(8,128)(2,1)S(1)}, u32[]{:S(2)}, u32[]{:S(2)}) collective-permute-start(bf16[576,128]{1,0:T(8,128)(2,1)S(1)} %get-tuple-element.25), channel_id=1, source_target_pairs={{0,1},{1,0},{2,3},{3,2},{4,5},{5,4},{6,7},{7,6},{8,9},{9,8},{10,11... | collective-permute-start | bytes 442376 | tf_op jit(solution)/shard_map/ppermute | solution.py:264
  27.8 2.2 %collective-permute-done.7.refs_6_ = bf16[288,128]{1,0:T(8,128)(2,1)S(1)} collective-permute-done((bf16[288,128]{1,0:T(8,128)(2,1)S(1)}, bf16[288,128]{1,0:T(8,128)(2,1)S(1)}, u32[]{:S(2)}, u32[]{:S(2)}) %collective-permute-start.7) | collective-permute-done | bytes 73760 | tf_op jit(solution)/shard_map/ppermute | solution.py:264
  30.0 0.7 %shard_map.81 = (bf16[288,128]{1,0:T(8,128)(2,1)S(1)}, bf16[2,12,24,128]{3,2,1,0:T(8,128)(2,1)S(1)}) custom-call(s32[8,128]{1,0:T(8,128)S(1)} %broadcast_in_dim.8.refs_0_, f32[4,288,128]{2,1,0:T(8,128)S(1)} %get-tuple-element.23.refs_1_, f32[4,288,128]{2,1,0:T(8,128)S(1)} %get-tuple-element.24.refs_2_, bf16[2,128,128]{2,1,0:T(8,128)(2,1)S(1)} %copy-done.5, ...), custom_call_target="tpu_custom_call" | custom-call | flops 2000000000 | bytes 1949696 | tf_op jit(solution)/shard_map/pallas_call | solution.py:84
  30.7 0.1 collective-permute-start.13
  30.8 0.7 %shard_map.83 = (bf16[288,128]{1,0:T(8,128)(2,1)S(1)}, bf16[2,12,24,128]{3,2,1,0:T(8,128)(2,1)S(1)}) custom-call(s32[8,128]{1,0:T(8,128)S(1)} %broadcast_in_dim.8.refs_0_, f32[4,288,128]{2,1,0:T(8,128)S(1)} %get-tuple-element.23.refs_1_, f32[4,288,128]{2,1,0:T(8,128)S(1)} %get-tuple-element.24.refs_2_, bf16[2,128,128]{2,1,0:T(8,128)(2,1)S(1)} %copy-done.5, ...), custom_call_target="tpu_custom_call" | custom-call | flops 2000000000 | bytes 1949696 | tf_op jit(solution)/shard_map/pallas_call | solution.py:84
  31.5 0.6 %collective-permute-start.14 = (bf16[2,12,24,128]{3,2,1,0:T(8,128)(2,1)S(1)}, bf16[2,12,24,128]{3,2,1,0:T(8,128)(2,1)S(1)}, u32[]{:S(2)}, u32[]{:S(2)}) collective-permute-start(bf16[2,12,24,128]{3,2,1,0:T(8,128)(2,1)S(1)} %get-tuple-element.40.refs_3_), channel_id=1, source_target_pairs={{0,2},{2,0},{4,6},{6,4},{8,10},{10,8},{12,14},{14,12},{1,3},{3,1},... | collective-permute-start | bytes 442376 | tf_op jit(solution)/shard_map/ppermute | solution.py:261
  32.0 0.3 collective-permute-done.4.refs_6_
  32.3 0.7 %shard_map.79 = (bf16[288,128]{1,0:T(8,128)(2,1)S(1)}, bf16[2,12,24,128]{3,2,1,0:T(8,128)(2,1)S(1)}) custom-call(s32[8,128]{1,0:T(8,128)S(1)} %broadcast_in_dim.8.refs_0_, f32[4,288,128]{2,1,0:T(8,128)S(1)} %get-tuple-element.23.refs_1_, f32[4,288,128]{2,1,0:T(8,128)S(1)} %get-tuple-element.24.refs_2_, bf16[2,128,128]{2,1,0:T(8,128)(2,1)S(1)} %copy-done.5, ...), custom_call_target="tpu_custom_call" | custom-call | flops 2000000000 | bytes 2023424 | tf_op jit(solution)/shard_map/pallas_call | solution.py:84
  32.9 0.1 collective-permute-start.12
  33.0 0.7 %shard_map.78 = (bf16[288,128]{1,0:T(8,128)(2,1)S(1)}, bf16[2,12,24,128]{3,2,1,0:T(8,128)(2,1)S(1)}) custom-call(s32[8,128]{1,0:T(8,128)S(1)} %broadcast_in_dim.8.refs_0_, f32[4,288,128]{2,1,0:T(8,128)S(1)} %get-tuple-element.23.refs_1_, f32[4,288,128]{2,1,0:T(8,128)S(1)} %get-tuple-element.24.refs_2_, bf16[2,128,128]{2,1,0:T(8,128)(2,1)S(1)} %copy-done.5, ...), custom_call_target="tpu_custom_call" | custom-call | flops 2000000000 | bytes 2023424 | tf_op jit(solution)/shard_map/pallas_call | solution.py:84
  33.7 0.6 %collective-permute-start.11 = (bf16[2,12,24,128]{3,2,1,0:T(8,128)(2,1)S(1)}, bf16[2,12,24,128]{3,2,1,0:T(8,128)(2,1)S(1)}, u32[]{:S(2)}, u32[]{:S(2)}) collective-permute-start(bf16[2,12,24,128]{3,2,1,0:T(8,128)(2,1)S(1)} %get-tuple-element.37.refs_0_), channel_id=1, source_target_pairs={{0,2},{2,0},{4,6},{6,4},{8,10},{10,8},{12,14},{14,12},{1,3},{3,1},... | collective-permute-start | bytes 442376 | tf_op jit(solution)/shard_map/ppermute | solution.py:261
  34.3 0.4 shard_map.84
  34.7 0.6 %collective-permute-done.11.refs_4_ = bf16[2,12,24,128]{3,2,1,0:T(8,128)(2,1)S(1)} collective-permute-done((bf16[2,12,24,128]{3,2,1,0:T(8,128)(2,1)S(1)}, bf16[2,12,24,128]{3,2,1,0:T(8,128)(2,1)S(1)}, u32[]{:S(2)}, u32[]{:S(2)}) %collective-permute-start.11) | collective-permute-done | bytes 147488 | tf_op jit(solution)/shard_map/ppermute | solution.py:261
  35.3 0.6 %shard_map.86 = bf16[12,48,128]{2,1,0:T(8,128)(2,1)S(1)} custom-call(bf16[2,12,24,128]{3,2,1,0:T(8,128)(2,1)S(1)} %get-tuple-element.37.refs_0_, bf16[2,12,24,128]{3,2,1,0:T(8,128)(2,1)S(1)} %get-tuple-element.38.refs_1_, bf16[2,12,24,128]{3,2,1,0:T(8,128)(2,1)S(1)} %get-tuple-element.39.refs_2_, bf16[2,12,24,128]{3,2,1,0:T(8,128)(2,1)S(1)} %get-tuple-element.40.refs_3_, ...), custom_call_target="tpu_custom_call" | custom-call | flops 2000000000 | bytes 1327104 | tf_op jit(solution)/shard_map/pallas_call | solution.py:84
  35.9 0.1 collective-permute-start.15
  36.0 0.6 %shard_map.87 = bf16[12,48,128]{2,1,0:T(8,128)(2,1)S(1)} custom-call(bf16[2,12,24,128]{3,2,1,0:T(8,128)(2,1)S(1)} %get-tuple-element.37.refs_0_, bf16[2,12,24,128]{3,2,1,0:T(8,128)(2,1)S(1)} %get-tuple-element.38.refs_1_, bf16[2,12,24,128]{3,2,1,0:T(8,128)(2,1)S(1)} %get-tuple-element.39.refs_2_, bf16[2,12,24,128]{3,2,1,0:T(8,128)(2,1)S(1)} %get-tuple-element.40.refs_3_, ...), custom_call_target="tpu_custom_call" | custom-call | flops 2000000000 | bytes 1327104 | tf_op jit(solution)/shard_map/pallas_call | solution.py:84
  36.6 3.1 %collective-permute-start.16 = (bf16[12,48,128]{2,1,0:T(8,128)(2,1)S(1)}, bf16[12,48,128]{2,1,0:T(8,128)(2,1)S(1)}, u32[]{:S(2)}, u32[]{:S(2)}) collective-permute-start(bf16[12,48,128]{2,1,0:T(8,128)(2,1)S(1)} %shard_map.87), channel_id=1, source_target_pairs={{0,8},{2,10},{4,12},{6,14},{8,0},{10,2},{12,4},{14,6},{1,9},{3,11}... | collective-permute-start | bytes 442376 | tf_op jit(solution)/shard_map/ppermute | solution.py:261
  39.7 0.6 %shard_map.88 = bf16[12,48,128]{2,1,0:T(8,128)(2,1)S(1)} custom-call(bf16[2,12,24,128]{3,2,1,0:T(8,128)(2,1)S(1)} %get-tuple-element.37.refs_0_, bf16[2,12,24,128]{3,2,1,0:T(8,128)(2,1)S(1)} %get-tuple-element.38.refs_1_, bf16[2,12,24,128]{3,2,1,0:T(8,128)(2,1)S(1)} %get-tuple-element.39.refs_2_, bf16[2,12,24,128]{3,2,1,0:T(8,128)(2,1)S(1)} %get-tuple-element.40.refs_3_, ...), custom_call_target="tpu_custom_call" | custom-call | flops 2000000000 | bytes 1327104 | tf_op jit(solution)/shard_map/pallas_call | solution.py:84
  40.3 0.0 copy-start.1
  40.3 0.0 copy-start.3
  40.3 1.4 %collective-permute-start.17 = (bf16[12,48,128]{2,1,0:T(8,128)(2,1)S(1)}, bf16[12,48,128]{2,1,0:T(8,128)(2,1)S(1)}, u32[]{:S(2)}, u32[]{:S(2)}) collective-permute-start(bf16[12,48,128]{2,1,0:T(8,128)(2,1)S(1)} %shard_map.88), channel_id=1, source_target_pairs={{0,12},{2,14},{4,8},{6,10},{8,4},{10,6},{12,0},{14,2},{1,13},{3,15... | collective-permute-start | bytes 442376 | tf_op jit(solution)/shard_map/ppermute | solution.py:261
  41.7 0.6 %shard_map.85.refs_6_ = f32[12,48,128]{2,1,0:T(8,128)S(1)} custom-call(bf16[2,12,24,128]{3,2,1,0:T(8,128)(2,1)S(1)} %get-tuple-element.37.refs_0_, bf16[2,12,24,128]{3,2,1,0:T(8,128)(2,1)S(1)} %get-tuple-element.38.refs_1_, bf16[2,12,24,128]{3,2,1,0:T(8,128)(2,1)S(1)} %get-tuple-element.39.refs_2_, bf16[2,12,24,128]{3,2,1,0:T(8,128)(2,1)S(1)} %get-tuple-element.40.refs_3_, ...), custom_call_target="tpu_custom_call" | custom-call | flops 2000000000 | bytes 1474560 | tf_op jit(solution)/shard_map/pallas_call | solution.py:84
  42.3 2.0 %collective-permute-done.15.refs_7_ = bf16[12,48,128]{2,1,0:T(8,128)(2,1)S(1)} collective-permute-done((bf16[12,48,128]{2,1,0:T(8,128)(2,1)S(1)}, bf16[12,48,128]{2,1,0:T(8,128)(2,1)S(1)}, u32[]{:S(2)}, u32[]{:S(2)}) %collective-permute-start.15) | collective-permute-done | bytes 147488 | tf_op jit(solution)/shard_map/ppermute | solution.py:261
  44.3 6.4 %collective-permute-done.16.refs_8_ = bf16[12,48,128]{2,1,0:T(8,128)(2,1)S(1)} collective-permute-done((bf16[12,48,128]{2,1,0:T(8,128)(2,1)S(1)}, bf16[12,48,128]{2,1,0:T(8,128)(2,1)S(1)}, u32[]{:S(2)}, u32[]{:S(2)}) %collective-permute-start.16) | collective-permute-done | bytes 147488 | tf_op jit(solution)/shard_map/ppermute | solution.py:261
  50.8 1.9 %shard_map.89 = bf16[12,48,128]{2,1,0:T(8,128)(2,1)} custom-call(s32[8,128]{1,0:T(8,128)S(1)} %broadcast_in_dim.8.refs_0_, bf16[12,48,128]{2,1,0:T(8,128)(2,1)S(1)} %get-tuple-element.35.refs_1_, f32[576,128]{1,0:T(8,128)S(1)} %get-tuple-element.36.refs_2_, bf16[2,128,128]{2,1,0:T(8,128)(2,1)S(1)} %copy-done.5, bf16[128,1024]{1,0:T(8,128)(2,1)S(1)} %copy-done.1, ...), custom_call_target="tpu_custom_call" | custom-call | flops 2000000000 | bytes 1785856 | tf_op jit(solution)/shard_map/pallas_call | solution.py:84
  (18 shorter events, 0.0 us)
Async XLA Ops:
  0.7 7.2 %copy-start.2 = (bf16[12,48,128]{2,1,0:T(8,128)(2,1)S(1)}, bf16[12,48,128]{2,1,0:T(8,128)(2,1)}, u32[]{:S(2)}) copy-start(bf16[12,48,128]{2,1,0:T(8,128)(2,1)} %refs_1_.5) | copy-start | bytes 442372
  0.7 8.9 %copy-start = (bf16[2,128,512]{2,1,0:T(8,128)(2,1)S(1)}, bf16[2,128,512]{2,1,0:T(8,128)(2,1)}, u32[]{:S(2)}) copy-start(bf16[2,128,512]{2,1,0:T(8,128)(2,1)} %refs_4_.8) | copy-start | bytes 786436
  2.1 9.9 %collective-permute-start.8 = (bf16[12,48,128]{2,1,0:T(8,128)(2,1)S(1)}, bf16[12,48,128]{2,1,0:T(8,128)(2,1)S(1)}, u32[]{:S(2)}, u32[]{:S(2)}) collective-permute-start(bf16[12,48,128]{2,1,0:T(8,128)(2,1)S(1)} %shard_map.75.refs_1_), channel_id=1, source_target_pairs={{0,12},{2,14},{4,8},{6,10},{8,4},{10,6},{12,0},{14,2},{1,13},{3,15... | collective-permute-start | bytes 442376 | tf_op jit(solution)/shard_map/ppermute | solution.py:261
  7.3 12.5 %collective-permute-start.5 = (bf16[12,48,128]{2,1,0:T(8,128)(2,1)S(1)}, bf16[12,48,128]{2,1,0:T(8,128)(2,1)S(1)}, u32[]{:S(2)}, u32[]{:S(2)}) collective-permute-start(bf16[12,48,128]{2,1,0:T(8,128)(2,1)S(1)} %shard_map.75.refs_1_), channel_id=1, source_target_pairs={{0,8},{2,10},{4,12},{6,14},{8,0},{10,2},{12,4},{14,6},{1,9},{3,11}... | collective-permute-start | bytes 442376 | tf_op jit(solution)/shard_map/ppermute | solution.py:261
  7.3 12.5 %collective-permute-start.2 = (bf16[12,48,128]{2,1,0:T(8,128)(2,1)S(1)}, bf16[12,48,128]{2,1,0:T(8,128)(2,1)S(1)}, u32[]{:S(2)}, u32[]{:S(2)}) collective-permute-start(bf16[12,48,128]{2,1,0:T(8,128)(2,1)S(1)} %shard_map.75.refs_1_), channel_id=1, source_target_pairs={{0,4},{2,6},{4,0},{6,2},{8,12},{10,14},{12,8},{14,10},{1,5},{3,7},... | collective-permute-start | bytes 442376 | tf_op jit(solution)/shard_map/ppermute | solution.py:261
  7.9 12.4 %collective-permute-start.1 = (bf16[12,48,128]{2,1,0:T(8,128)(2,1)S(1)}, bf16[12,48,128]{2,1,0:T(8,128)(2,1)S(1)}, u32[]{:S(2)}, u32[]{:S(2)}) collective-permute-start(bf16[12,48,128]{2,1,0:T(8,128)(2,1)S(1)} %shard_map.75.refs_1_), channel_id=1, source_target_pairs={{0,2},{2,0},{4,6},{6,4},{8,10},{10,8},{12,14},{14,12},{1,3},{3,1},... | collective-permute-start | bytes 442376 | tf_op jit(solution)/shard_map/ppermute | solution.py:261
  7.9 13.1 %collective-permute-start = (bf16[12,48,128]{2,1,0:T(8,128)(2,1)S(1)}, bf16[12,48,128]{2,1,0:T(8,128)(2,1)S(1)}, u32[]{:S(2)}, u32[]{:S(2)}) collective-permute-start(bf16[12,48,128]{2,1,0:T(8,128)(2,1)S(1)} %copy-done.2), channel_id=1, source_target_pairs={{0,1},{1,0},{2,3},{3,2},{4,5},{5,4},{6,7},{7,6},{8,9},{9,8},{10,11... | collective-permute-start | bytes 442376 | tf_op jit(solution)/shard_map/ppermute | solution.py:264
  10.0 11.1 %copy-start.4 = (bf16[2,128,128]{2,1,0:T(8,128)(2,1)S(1)}, bf16[2,128,128]{2,1,0:T(8,128)(2,1)}, u32[]{:S(2)}) copy-start(bf16[2,128,128]{2,1,0:T(8,128)(2,1)} %refs_0_.3) | copy-start | bytes 196612
  12.1 9.5 %collective-permute-start.9 = (bf16[12,48,128]{2,1,0:T(8,128)(2,1)S(1)}, bf16[12,48,128]{2,1,0:T(8,128)(2,1)S(1)}, u32[]{:S(2)}, u32[]{:S(2)}) collective-permute-start(bf16[12,48,128]{2,1,0:T(8,128)(2,1)S(1)} %collective-permute-done.8.refs_1_), channel_id=1, source_target_pairs={{0,2},{2,0},{4,6},{6,4},{8,10},{10,8},{12,14},{14,12},{1,3},{3,1},... | collective-permute-start | bytes 442376 | tf_op jit(solution)/shard_map/ppermute | solution.py:261
  19.7 4.2 %collective-permute-start.6 = (bf16[12,48,128]{2,1,0:T(8,128)(2,1)S(1)}, bf16[12,48,128]{2,1,0:T(8,128)(2,1)S(1)}, u32[]{:S(2)}, u32[]{:S(2)}) collective-permute-start(bf16[12,48,128]{2,1,0:T(8,128)(2,1)S(1)} %collective-permute-done.5.refs_1_), channel_id=1, source_target_pairs={{0,2},{2,0},{4,6},{6,4},{8,10},{10,8},{12,14},{14,12},{1,3},{3,1},... | collective-permute-start | bytes 442376 | tf_op jit(solution)/shard_map/ppermute | solution.py:261
  19.7 5.6 %collective-permute-start.3 = (bf16[12,48,128]{2,1,0:T(8,128)(2,1)S(1)}, bf16[12,48,128]{2,1,0:T(8,128)(2,1)S(1)}, u32[]{:S(2)}, u32[]{:S(2)}) collective-permute-start(bf16[12,48,128]{2,1,0:T(8,128)(2,1)S(1)} %collective-permute-done.2.refs_1_), channel_id=1, source_target_pairs={{0,2},{2,0},{4,6},{6,4},{8,10},{10,8},{12,14},{14,12},{1,3},{3,1},... | collective-permute-start | bytes 442376 | tf_op jit(solution)/shard_map/ppermute | solution.py:261
  22.4 8.3 %collective-permute-start.10 = (bf16[288,128]{1,0:T(8,128)(2,1)S(1)}, bf16[288,128]{1,0:T(8,128)(2,1)S(1)}, u32[]{:S(2)}, u32[]{:S(2)}) collective-permute-start(bf16[288,128]{1,0:T(8,128)(2,1)S(1)} %get-tuple-element.33), channel_id=1, source_target_pairs={{0,1},{1,0},{2,3},{3,2},{4,5},{5,4},{6,7},{7,6},{8,9},{9,8},{10,11... | collective-permute-start | bytes 221192 | tf_op jit(solution)/shard_map/ppermute | solution.py:264
  24.8 5.2 %copy-start.5 = (bf16[2,128,128]{2,1,0:T(8,128)(2,1)S(1)}, bf16[2,128,128]{2,1,0:T(8,128)(2,1)}, u32[]{:S(2)}) copy-start(bf16[2,128,128]{2,1,0:T(8,128)(2,1)} %refs_3_.9) | copy-start | bytes 196612
  24.8 5.2 %collective-permute-start.7 = (bf16[288,128]{1,0:T(8,128)(2,1)S(1)}, bf16[288,128]{1,0:T(8,128)(2,1)S(1)}, u32[]{:S(2)}, u32[]{:S(2)}) collective-permute-start(bf16[288,128]{1,0:T(8,128)(2,1)S(1)} %get-tuple-element.30), channel_id=1, source_target_pairs={{0,1},{1,0},{2,3},{3,2},{4,5},{5,4},{6,7},{7,6},{8,9},{9,8},{10,11... | collective-permute-start | bytes 221192 | tf_op jit(solution)/shard_map/ppermute | solution.py:264
  26.2 6.1 %collective-permute-start.4 = (bf16[576,128]{1,0:T(8,128)(2,1)S(1)}, bf16[576,128]{1,0:T(8,128)(2,1)S(1)}, u32[]{:S(2)}, u32[]{:S(2)}) collective-permute-start(bf16[576,128]{1,0:T(8,128)(2,1)S(1)} %get-tuple-element.25), channel_id=1, source_target_pairs={{0,1},{1,0},{2,3},{3,2},{4,5},{5,4},{6,7},{7,6},{8,9},{9,8},{10,11... | collective-permute-start | bytes 442376 | tf_op jit(solution)/shard_map/ppermute | solution.py:264
  30.7 4.0 %collective-permute-start.13 = (bf16[2,12,24,128]{3,2,1,0:T(8,128)(2,1)S(1)}, bf16[2,12,24,128]{3,2,1,0:T(8,128)(2,1)S(1)}, u32[]{:S(2)}, u32[]{:S(2)}) collective-permute-start(bf16[2,12,24,128]{3,2,1,0:T(8,128)(2,1)S(1)} %get-tuple-element.39.refs_2_), channel_id=1, source_target_pairs={{0,2},{2,0},{4,6},{6,4},{8,10},{10,8},{12,14},{14,12},{1,3},{3,1},... | collective-permute-start | bytes 442376 | tf_op jit(solution)/shard_map/ppermute | solution.py:261
  31.5 3.2 %collective-permute-start.14 = (bf16[2,12,24,128]{3,2,1,0:T(8,128)(2,1)S(1)}, bf16[2,12,24,128]{3,2,1,0:T(8,128)(2,1)S(1)}, u32[]{:S(2)}, u32[]{:S(2)}) collective-permute-start(bf16[2,12,24,128]{3,2,1,0:T(8,128)(2,1)S(1)} %get-tuple-element.40.refs_3_), channel_id=1, source_target_pairs={{0,2},{2,0},{4,6},{6,4},{8,10},{10,8},{12,14},{14,12},{1,3},{3,1},... | collective-permute-start | bytes 442376 | tf_op jit(solution)/shard_map/ppermute | solution.py:261
  32.9 1.7 %collective-permute-start.12 = (bf16[2,12,24,128]{3,2,1,0:T(8,128)(2,1)S(1)}, bf16[2,12,24,128]{3,2,1,0:T(8,128)(2,1)S(1)}, u32[]{:S(2)}, u32[]{:S(2)}) collective-permute-start(bf16[2,12,24,128]{3,2,1,0:T(8,128)(2,1)S(1)} %get-tuple-element.38.refs_1_), channel_id=1, source_target_pairs={{0,2},{2,0},{4,6},{6,4},{8,10},{10,8},{12,14},{14,12},{1,3},{3,1},... | collective-permute-start | bytes 442376 | tf_op jit(solution)/shard_map/ppermute | solution.py:261
  33.7 1.6 %collective-permute-start.11 = (bf16[2,12,24,128]{3,2,1,0:T(8,128)(2,1)S(1)}, bf16[2,12,24,128]{3,2,1,0:T(8,128)(2,1)S(1)}, u32[]{:S(2)}, u32[]{:S(2)}) collective-permute-start(bf16[2,12,24,128]{3,2,1,0:T(8,128)(2,1)S(1)} %get-tuple-element.37.refs_0_), channel_id=1, source_target_pairs={{0,2},{2,0},{4,6},{6,4},{8,10},{10,8},{12,14},{14,12},{1,3},{3,1},... | collective-permute-start | bytes 442376 | tf_op jit(solution)/shard_map/ppermute | solution.py:261
  35.9 8.4 %collective-permute-start.15 = (bf16[12,48,128]{2,1,0:T(8,128)(2,1)S(1)}, bf16[12,48,128]{2,1,0:T(8,128)(2,1)S(1)}, u32[]{:S(2)}, u32[]{:S(2)}) collective-permute-start(bf16[12,48,128]{2,1,0:T(8,128)(2,1)S(1)} %shard_map.86), channel_id=1, source_target_pairs={{0,4},{2,6},{4,0},{6,2},{8,12},{10,14},{12,8},{14,10},{1,5},{3,7},... | collective-permute-start | bytes 442376 | tf_op jit(solution)/shard_map/ppermute | solution.py:261
  36.6 14.2 %collective-permute-start.16 = (bf16[12,48,128]{2,1,0:T(8,128)(2,1)S(1)}, bf16[12,48,128]{2,1,0:T(8,128)(2,1)S(1)}, u32[]{:S(2)}, u32[]{:S(2)}) collective-permute-start(bf16[12,48,128]{2,1,0:T(8,128)(2,1)S(1)} %shard_map.87), channel_id=1, source_target_pairs={{0,8},{2,10},{4,12},{6,14},{8,0},{10,2},{12,4},{14,6},{1,9},{3,11}... | collective-permute-start | bytes 442376 | tf_op jit(solution)/shard_map/ppermute | solution.py:261
  40.3 10.5 %copy-start.1 = (bf16[128,1024]{1,0:T(8,128)(2,1)S(1)}, bf16[128,1024]{1,0:T(8,128)(2,1)}, u32[]{:S(2)}) copy-start(bf16[128,1024]{1,0:T(8,128)(2,1)} %refs_4_.9) | copy-start | bytes 786436
  40.3 10.4 %copy-start.3 = (bf16[512,128]{1,0:T(8,128)(2,1)S(1)}, bf16[512,128]{1,0:T(8,128)(2,1)}, u32[]{:S(2)}) copy-start(bf16[512,128]{1,0:T(8,128)(2,1)} %refs_5_.1) | copy-start | bytes 393220
  40.3 10.4 %collective-permute-start.17 = (bf16[12,48,128]{2,1,0:T(8,128)(2,1)S(1)}, bf16[12,48,128]{2,1,0:T(8,128)(2,1)S(1)}, u32[]{:S(2)}, u32[]{:S(2)}) collective-permute-start(bf16[12,48,128]{2,1,0:T(8,128)(2,1)S(1)} %shard_map.88), channel_id=1, source_target_pairs={{0,12},{2,14},{4,8},{6,10},{8,4},{10,6},{12,0},{14,2},{1,13},{3,15... | collective-permute-start | bytes 442376 | tf_op jit(solution)/shard_map/ppermute | solution.py:261
